TPU v7x, 128 devices: a whole 4x4x4 slice. The times are simulated.
128 devices in a mesh: seq: 8 (over z, core), grp: 16 (over x, y).
Axes of the slice: x: 4, y: 4, z: 4, core: 2. Of those that a mesh axis runs over, the one named last changes fastest.
Arguments:
- qkv: bfloat16 [16384, 3, 2048], P(('seq', 'grp')), may hold values from -6 to 6
- cluster_lists: int32 [16, 16, 1024], P('seq', 'grp'), may hold values from 0 to 16383, as said below
- w_out: bfloat16 [2048, 2048], replicated, may hold values from -0.125 to 0.125
- norm_gain: bfloat16 [2048], replicated, may hold values from 0.099609375 to 1.8984375
- router: bfloat16 [2048, 128], replicated, may hold values from -0.125 to 0.125
- expert_lists: int32 [128, 512], replicated, may hold values from 0 to 16383, as said below
- w_gate: bfloat16 [128, 2048, 768], P(('seq', 'grp')), may hold values from -0.125 to 0.125
- w_up: bfloat16 [128, 2048, 768], P(('seq', 'grp')), may hold values from -0.125 to 0.125
- w_down: bfloat16 [128, 768, 2048], P(('seq', 'grp')), may hold values from -0.21875 to 0.21875
Outputs:
- layer_out: bfloat16 [16384, 2048], P(('seq', 'grp'))
Inputs may be any that keep to these rules, and one draw needn't show every extreme that they name: `cluster_lists`: within each head the 16 lists are disjoint, each ascending, and together hold every one of the 16384 tokens once. Of the 128 tokens of an aligned block, one list holds at most 12, and for every head some list holds exactly 12. `expert_lists`: each list is ascending with distinct rows. Of the 128 rows of an aligned block, one list holds at most 6, and some list holds exactly 6.
All inputs are finite; a program needn't handle non-finite values.
Results may differ from a plain program's by a relative error of at most 0.019.
Values may be sent and summed in bfloat16 or wider, within the bound.
No kernel may reach another device: no remote copies, remote signals or barrier semaphores. Data moves between devices by JAX's collectives and lax.ppermute only.
A program may use at most 128 MiB of HBM per device.

v0:
```python
import jax
import jax.numpy as jnp
from jax import lax
from jax.experimental import pallas as pl
from jax.experimental.pallas import tpu as pltpu
from jax.sharding import PartitionSpec as P

BF16 = jnp.bfloat16
F32 = jnp.float32
I32 = jnp.int32
ALL = ("seq", "grp")

SEQ = 8
GRP = 16
DEVICES = 128
ROWS = 128
HEAD = 128
WIDTH = 2048
CHUNKS = WIDTH // 128
CLUSTER = 1024
SLOTS = 12
LOW = 8
HIGH = 4
ESLOTS = 6
CHOSEN = 512
HIDDEN = 768
SENT = DEVICES * ESLOTS
GROUP = 32
GROWS = GROUP * SLOTS
PLACES = DEVICES * SLOTS

NN = (((1,), (0,)), ((), ()))
NT = (((1,), (1,)), ((), ()))
TN = (((0,), (0,)), ((), ()))
VMEM_LIMIT = 60 * 1024 * 1024


def iota(shape, axis):
    return lax.broadcasted_iota(I32, shape, axis)


def dot(a, b, dims=NN):
    return lax.dot_general(a, b, dims, preferred_element_type=F32)


def whole(space=pltpu.VMEM):
    return pl.BlockSpec(memory_space=space)


def rank_in_block(block, most):
    lane = iota(block.shape, 1)
    rank = jnp.zeros(block.shape, I32)
    for back in range(1, most):
        same = (pltpu.roll(block, back, 1) == block) & (lane >= back)
        rank = rank + jnp.where(same, 1, 0)
    return rank


def request_kernel(place_ref, lists_ref, out_ref):
    grp = place_ref[1]
    line = iota((128, CLUSTER), 0)
    high = jnp.zeros((DEVICES, 128), F32)
    for h in range(2):
        token = lists_ref[h]
        block = token >> 7
        rank = rank_in_block(block, SLOTS)
        row = ((token & 127) + 1).astype(F32)
        member = jnp.where(block == line, 1.0, 0.0).astype(BF16)
        low_line = jnp.where(rank < LOW, grp * LOW + rank, -1)
        high_line = jnp.where(rank < LOW, -1, grp * LOW + HIGH * h + rank - LOW)
        low_rows = jnp.where(low_line == line, row, 0.0).astype(BF16)
        high_rows = jnp.where(high_line == line, row, 0.0).astype(BF16)
        out_ref[:, h, :] = dot(member, low_rows, NT)
        high = high + dot(member, high_rows, NT)
    out_ref[:, 2, :] = high
    out_ref[:, 3, :] = jnp.zeros((DEVICES, 128), F32)


def place_order(index):
    group = index // GROWS
    inner = index - group * GROWS
    upper = inner - GROUP * LOW
    is_low = inner < GROUP * LOW
    source = group * GROUP + jnp.where(is_low, inner >> 3, upper >> 2)
    slot = jnp.where(is_low, inner & 7, LOW + (upper & 3))
    return source, slot


def order_kernel(lists_ref, out_ref):
    line = iota((128, CLUSTER), 0)
    source, slot = place_order(iota((1, PLACES), 1))
    spread = jnp.where(iota((128, PLACES), 0) == source, 1.0, 0.0).astype(BF16)
    key = (source * SLOTS + slot).astype(F32)
    for h in range(2):
        member = jnp.where((lists_ref[h] >> 7) == line, 1.0, 0.0).astype(BF16)
        count = dot(jnp.ones((8, CLUSTER), BF16), member, NT)
        held = dot(count.astype(BF16), spread)
        out_ref[h] = jnp.where(slot.astype(F32) < held, key, 1e9)


def expert_index_kernel(place_ref, lists_ref, rows_ref, slots_ref):
    me = place_ref[0]
    lists = lists_ref[...]
    inside = (lists >> 7) == me
    position = iota((DEVICES, CHOSEN), 1)
    before = jnp.sum(jnp.where(lists < me * ROWS, 1.0, 0.0), axis=1, keepdims=True).astype(I32)
    row = (lists - me * ROWS + 1).astype(F32)
    rank = jnp.where(inside, position - before, -1)
    lane = iota((DEVICES, 128), 1)
    rows = jnp.zeros((DEVICES, 128), F32)
    for k in range(ESLOTS):
        found = jnp.sum(jnp.where(rank == k, row, 0.0), axis=1, keepdims=True)
        rows = jnp.where(lane == k, found, rows)
    rows_ref[...] = rows.astype(I32)
    mine = lists_ref[pl.ds(me, 1), :]
    block = mine >> 7
    slots_ref[...] = block * ESLOTS + rank_in_block(block, ESLOTS)


def select_kernel(request_ref, qkv_ref, out_ref):
    rows = jnp.sum(request_ref[...], axis=0)
    token = (iota((ROWS, 128), 0) + 1).astype(F32)
    lane_head = (iota((ROWS, 128), 1) >> 2) & 1
    high_match = rows[2:3, :] == token
    high = jnp.zeros((128, 3 * HEAD), F32)
    for h in range(2):
        columns = slice(h * HEAD, (h + 1) * HEAD)
        packed = jnp.concatenate([qkv_ref[c, :, columns] for c in range(3)], axis=1)
        low_match = jnp.where(rows[h : h + 1, :] == token, 1.0, 0.0).astype(BF16)
        low = dot(low_match, packed, TN).astype(BF16)
        mine = jnp.where(high_match & (lane_head == h), 1.0, 0.0).astype(BF16)
        high = high + dot(mine, packed, TN)
        for c in range(3):
            out_ref[:, h * 3 + c] = low[:, c * HEAD : (c + 1) * HEAD].reshape(GRP, 8, HEAD)
    high = high.astype(BF16)
    for c in range(3):
        out_ref[:, 6 + c] = high[:, c * HEAD : (c + 1) * HEAD].reshape(GRP, 8, HEAD)


def attend_kernel(order_ref, x_ref, out_ref, packed_ref):
    scale = HEAD ** (-0.5)
    low_rows = GROUP * LOW
    high_rows = GROUP * HIGH
    joint = iota((2 * high_rows, high_rows), 0)
    apart = iota((2 * high_rows, high_rows), 1)
    same_place = (joint >> 3) * HIGH + (joint & 3) == apart
    spread = [
        jnp.where(same_place & (((joint >> 2) & 1) == h), 1.0, 0.0).astype(BF16) for h in range(2)
    ]
    groups = DEVICES // GROUP
    for i in range(groups):
        blocks = slice(i * GROUP, (i + 1) * GROUP)
        for c in range(3):
            both = x_ref[blocks, 6 + c].reshape(2 * high_rows, HEAD)
            for h in range(2):
                start = i * GROWS
                packed_ref[h, c, start : start + low_rows, :] = x_ref[blocks, h * 3 + c].reshape(
                    low_rows, HEAD
                )
                packed_ref[h, c, start + low_rows : start + GROWS, :] = dot(
                    spread[h], both, TN
                ).astype(BF16)
    for i in range(groups):
        blocks = slice(i * GROUP, (i + 1) * GROUP)
        seen = (i + 1) * GROWS
        source, slot = place_order(i * GROWS + iota((GROWS, 1), 0))
        query_order = (source * SLOTS + slot).astype(F32)
        joined = jnp.zeros((2 * high_rows, HEAD), F32)
        for h in range(2):
            queries = packed_ref[h, 0, i * GROWS : seen, :]
            scores = dot(queries, packed_ref[h, 1, :seen, :], NT) * scale
            key_order = order_ref[h, 0:1, :seen]
            scores = jnp.where(key_order <= query_order, scores, -1e30)
            top = jnp.max(scores, axis=1, keepdims=True)
            grown = jnp.exp(scores - top)
            totals = jnp.sum(grown, axis=1, keepdims=True)
            summed = dot(grown.astype(BF16), packed_ref[h, 2, :seen, :])
            result = (summed / totals).astype(BF16)
            out_ref[blocks, h] = result[:low_rows].reshape(GROUP, 8, HEAD)
            joined = joined + dot(spread[h], result[low_rows:])
        out_ref[blocks, 2] = joined.astype(BF16).reshape(GROUP, 8, HEAD)


def mix_kernel(
    rows_ref, request_ref, came_ref, w_out_ref, gain_ref, mixed_ref, out_ref, w_ref, att_ref, tall_ref, tile_ref, sems
):
    parts = sems.shape[0]
    depth = WIDTH // parts
    copies = [
        pltpu.make_async_copy(
            w_out_ref.at[pl.ds(p * depth, depth), :], w_ref.at[pl.ds(p * depth, depth), :], sems.at[p]
        )
        for p in range(parts)
    ]
    for copy in copies:
        copy.start()
    token = (iota((ROWS, 128), 0) + 1).astype(F32)
    lane_head = (iota((ROWS, 128), 1) >> 2) & 1
    for s in range(SEQ):
        peers = slice(s * GRP, (s + 1) * GRP)
        rows = jnp.sum(request_ref[peers], axis=0)
        high_match = rows[2:3, :] == token
        high = came_ref[peers, 2].reshape(128, HEAD)
        for h in range(2):
            low_match = jnp.where(rows[h : h + 1, :] == token, 1.0, 0.0).astype(BF16)
            mine = jnp.where(high_match & (lane_head == h), 1.0, 0.0).astype(BF16)
            got = dot(low_match, came_ref[peers, h].reshape(128, HEAD)) + dot(mine, high)
            start = (2 * s + h) * HEAD
            att_ref[:, start : start + HEAD] = got.astype(BF16)
    total = jnp.zeros((ROWS, WIDTH), F32)
    for p in range(parts):
        copies[p].wait()
        total = total + dot(
            att_ref[:, p * depth : (p + 1) * depth], w_ref[p * depth : (p + 1) * depth, :]
        )
    mixed = total.astype(BF16)
    mixed_ref[...] = mixed
    wide = mixed.astype(F32)
    mean_square = jnp.mean(wide * wide, axis=1, keepdims=True)
    normed = wide * lax.rsqrt(mean_square + 1e-06) * gain_ref[...].astype(F32)
    for j in range(CHUNKS):
        tall_ref[pl.ds(j, ROWS, stride=CHUNKS), :] = normed[:, j * 128 : (j + 1) * 128]
    tile_ref[...] = tall_ref[...].astype(BF16).reshape(ROWS, CHUNKS, 128)

    def send(e, carry):
        for k in range(ESLOTS):
            out_ref[e * ESLOTS + k] = tile_ref[jnp.maximum(rows_ref[e, k] - 1, 0)]
        return carry

    lax.fori_loop(0, DEVICES, send, 0)


def expert_kernel(
    place_ref, slots_ref, x_ref, gate_hbm, up_hbm, down_hbm, router_ref, out_ref,
    gate_ref, up_ref, down_ref, tall_ref, rows_ref, sems,
):
    copies = [
        pltpu.make_async_copy(source.at[0], target, sems.at[n])
        for n, (source, target) in enumerate(
            [(gate_hbm, gate_ref), (up_hbm, up_ref), (down_hbm, down_ref)]
        )
    ]
    for copy in copies:
        copy.start()
    half = rows_ref.shape[0]
    me = place_ref[0]
    for part in range(CHOSEN // half):
        base = part * half

        def take(i, carry):
            for n in range(8):
                at = i * 8 + n
                tall_ref[pl.ds(pl.multiple_of(at * CHUNKS, CHUNKS), CHUNKS), :] = x_ref[
                    slots_ref[0, base + at]
                ].astype(F32)
            return carry

        lax.fori_loop(0, half // 8, take, 0)
        for j in range(CHUNKS):
            rows_ref[:, j * 128 : (j + 1) * 128] = tall_ref[pl.ds(j, half, stride=CHUNKS), :].astype(BF16)
        rows = rows_ref[...]
        logits = dot(rows, router_ref[...])
        mine = jnp.where(iota((half, 128), 1) == me, logits, 0.0)
        weight = jax.nn.sigmoid(jnp.sum(mine, axis=1, keepdims=True))
        if part == 0:
            copies[0].wait()
        gate = dot(rows, gate_ref[...])
        if part == 0:
            copies[1].wait()
        up = dot(rows, up_ref[...])
        hidden = (jax.nn.silu(gate) * up).astype(BF16)
        if part == 0:
            copies[2].wait()
        result = dot(hidden, down_ref[...]) * weight
        for j in range(CHUNKS):
            tall_ref[pl.ds(j, half, stride=CHUNKS), :] = result[:, j * 128 : (j + 1) * 128]

        def put(i, carry):
            for n in range(8):
                at = i * 8 + n
                out_ref[slots_ref[0, base + at]] = tall_ref[
                    pl.ds(pl.multiple_of(at * CHUNKS, CHUNKS), CHUNKS), :
                ].astype(BF16)
            return carry

        lax.fori_loop(0, half // 8, put, 0)


def combine_kernel(rows_ref, mixed_ref, x_ref, out_ref, tall_ref, flat_ref):
    token = iota((DEVICES, ROWS), 1) + 1
    total = mixed_ref[...].astype(F32)
    for k in range(ESLOTS):

        def take(i, carry):
            for n in range(8):
                e = i * 8 + n
                tall_ref[pl.ds(pl.multiple_of(e * CHUNKS, CHUNKS), CHUNKS), :] = x_ref[
                    e * ESLOTS + k
                ].astype(F32)
            return carry

        lax.fori_loop(0, DEVICES // 8, take, 0)
        for j in range(CHUNKS):
            flat_ref[:, j * 128 : (j + 1) * 128] = tall_ref[
                pl.ds(j, DEVICES, stride=CHUNKS), :
            ].astype(BF16)
        held = rows_ref[:, k : k + 1]
        kept = jnp.where(held > 0, flat_ref[...].astype(F32), 0.0).astype(BF16)
        match = jnp.where(held == token, 1.0, 0.0).astype(BF16)
        total = total + dot(match, kept, TN)
    out_ref[...] = total.astype(BF16)


def call(kernel, out_shape, in_specs, scratch=(), **kwargs):
    return pl.pallas_call(
        kernel,
        out_shape=out_shape,
        in_specs=in_specs,
        out_specs=jax.tree.map(lambda _: whole(), out_shape),
        scratch_shapes=list(scratch),
        compiler_params=pltpu.CompilerParams(vmem_limit_bytes=VMEM_LIMIT),
        **kwargs,
    )


def shape(dims, dtype=BF16):
    return jax.ShapeDtypeStruct(dims, dtype)


def exchange(array):
    return lax.all_to_all(array, ALL, split_axis=0, concat_axis=0, tiled=True)


def shards(qkv, cluster_lists, w_out, norm_gain, router, expert_lists, w_gate, w_up, w_down):
    grp = lax.axis_index("grp")
    place = jnp.stack([lax.axis_index("seq") * GRP + grp, grp]).astype(I32)
    smem = whole(pltpu.SMEM)
    hbm = whole(pl.ANY)

    request = call(request_kernel, shape((DEVICES, 4, 128), F32), [smem, whole()])(place, cluster_lists)
    asked = exchange(request)
    order = call(order_kernel, shape((2, 8, PLACES), F32), [whole()])(cluster_lists)
    rows, slots = call(
        expert_index_kernel,
        (shape((DEVICES, 128), I32), shape((1, CHOSEN), I32)),
        [smem, whole()],
    )(place, expert_lists)

    picked = pl.pallas_call(
        select_kernel,
        out_shape=shape((DEVICES, 9, 8, HEAD)),
        grid=(SEQ,),
        in_specs=[
            pl.BlockSpec((GRP, 4, 128), lambda s: (s, 0, 0)),
            pl.BlockSpec((3, ROWS, 2 * HEAD), lambda s: (0, 0, s)),
        ],
        out_specs=pl.BlockSpec((GRP, 9, 8, HEAD), lambda s: (s, 0, 0, 0)),
    )(asked, qkv.transpose(1, 0, 2))
    arrived = exchange(picked)

    outputs = call(
        attend_kernel,
        shape((DEVICES, 3, 8, HEAD)),
        [whole(), whole()],
        [pltpu.VMEM((2, 3, PLACES, HEAD), BF16)],
    )(order, arrived)
    came_back = exchange(outputs)

    mixed, outgoing = call(
        mix_kernel,
        (shape((ROWS, WIDTH)), shape((SENT, CHUNKS, 128))),
        [smem, whole(), whole(), hbm, whole()],
        [
            pltpu.VMEM((WIDTH, WIDTH), BF16),
            pltpu.VMEM((ROWS, WIDTH), BF16),
            pltpu.VMEM((ROWS * CHUNKS, 128), F32),
            pltpu.VMEM((ROWS, CHUNKS, 128), BF16),
            pltpu.SemaphoreType.DMA((4,)),
        ],
    )(rows, asked, came_back, w_out, norm_gain.reshape(1, WIDTH))
    incoming = exchange(outgoing)

    half = CHOSEN // 2
    produced = call(
        expert_kernel,
        shape((SENT, CHUNKS, 128)),
        [smem, smem, whole(), hbm, hbm, hbm, whole()],
        [
            pltpu.VMEM((WIDTH, HIDDEN), BF16),
            pltpu.VMEM((WIDTH, HIDDEN), BF16),
            pltpu.VMEM((HIDDEN, WIDTH), BF16),
            pltpu.VMEM((half * CHUNKS, 128), F32),
            pltpu.VMEM((half, WIDTH), BF16),
            pltpu.SemaphoreType.DMA((3,)),
        ],
    )(place, slots, incoming, w_gate, w_up, w_down, router)
    results = exchange(produced)

    return call(
        combine_kernel,
        shape((ROWS, WIDTH)),
        [whole(), whole(), whole()],
        [pltpu.VMEM((DEVICES * CHUNKS, 128), F32), pltpu.VMEM((DEVICES, WIDTH), BF16)],
    )(rows, mixed, results)


def solution(mesh):
    return jax.shard_map(
        shards,
        mesh=mesh,
        in_specs=(
            P(("seq", "grp"), None, None),
            P("seq", "grp", None),
            P(),
            P(),
            P(),
            P(),
            P(("seq", "grp"), None, None),
            P(("seq", "grp"), None, None),
            P(("seq", "grp"), None, None),
        ),
        out_specs=P(("seq", "grp"), None),
        check_vma=False,
    )
```

profile of v0, /device:TPU:1, one launch (start us, length us, event | category | flops | bytes accessed | tf_op | source)
XLA Modules:
  0.0 227.1 jit_solution(3365671475072523033)
XLA Ops:
  0.0 0.6 pad_add_fusion.place_ref
  0.6 2.2 shard_map.92
  2.8 22.7 %all_to_all.25.request_ref = f32[128,4,128]{2,1,0:T(4,128)} all-to-all(f32[128,4,128]{2,1,0:T(4,128)} %shard_map.92), channel_id=1, replica_groups=mesh['seq'=8,'grp'=16] {'seq','grp'}, dimensions={0} | all-to-all | bytes 524288 | tf_op jit(solution)/shard_map/all_to_all | solution.py:331
  25.6 6.8 %shard_map.94 = bf16[128,9,8,128]{3,2,1,0:T(8,128)(2,1)} custom-call(f32[128,4,128]{2,1,0:T(4,128)} %all_to_all.25.request_ref, bf16[3,128,2048]{2,1,0:T(8,128)(2,1)} %bitcast.3), custom_call_target="tpu_custom_call" | custom-call | tf_op jit(solution)/shard_map/pallas_call | solution.py:349
  32.4 4.3 %all-to-all-start.1 = ((bf16[128,9,8,128]{3,2,1,0:T(8,128)(2,1)}), bf16[128,9,8,128]{3,2,1,0:T(8,128)(2,1)S(1)}, u32[]{:S(2)}, u32[]{:S(2)}) async-start(bf16[128,9,8,128]{3,2,1,0:T(8,128)(2,1)} %shard_map.94), calls=%async_computation.1 | async-start | bytes 4718592 | tf_op jit(solution)/shard_map/all_to_all | solution.py:331
  36.6 0.0 copy-start.2
  36.7 2.1 shard_map.93.order_ref
  38.8 30.5 %all-to-all-done.1.x_ref = bf16[128,9,8,128]{3,2,1,0:T(8,128)(2,1)S(1)} async-done(((bf16[128,9,8,128]{3,2,1,0:T(8,128)(2,1)}), bf16[128,9,8,128]{3,2,1,0:T(8,128)(2,1)S(1)}, u32[]{:S(2)}, u32[]{:S(2)}) %all-to-all-start.1) | async-done | bytes 2359328 | tf_op jit(solution)/shard_map/all_to_all | solution.py:331
  69.3 0.0 copy-start
  69.3 1.4 copy-done
  70.7 10.2 %shard_map.95 = bf16[128,3,8,128]{3,2,1,0:T(8,128)(2,1)} custom-call(f32[2,8,1536]{2,1,0:T(8,128)} %shard_map.93.order_ref, bf16[128,9,8,128]{3,2,1,0:T(8,128)(2,1)} %copy-done), custom_call_target="tpu_custom_call" | custom-call | tf_op jit(solution)/shard_map/pallas_call | solution.py:361
  81.0 4.5 %all-to-all-start.2 = ((bf16[128,3,8,128]{3,2,1,0:T(8,128)(2,1)}), bf16[128,3,8,128]{3,2,1,0:T(8,128)(2,1)S(1)}, u32[]{:S(2)}, u32[]{:S(2)}) async-start(bf16[128,3,8,128]{3,2,1,0:T(8,128)(2,1)} %shard_map.95), calls=%async_computation.2 | async-start | bytes 1572864 | tf_op jit(solution)/shard_map/all_to_all | solution.py:331
  85.5 0.0 copy-done.2
  85.5 0.6 reshape.3.gain_ref
  86.1 2.0 shard_map.91
  88.1 13.5 %all-to-all-done.2.came_ref = bf16[128,3,8,128]{3,2,1,0:T(8,128)(2,1)S(1)} async-done(((bf16[128,3,8,128]{3,2,1,0:T(8,128)(2,1)}), bf16[128,3,8,128]{3,2,1,0:T(8,128)(2,1)S(1)}, u32[]{:S(2)}, u32[]{:S(2)}) %all-to-all-start.2) | async-done | bytes 786464 | tf_op jit(solution)/shard_map/all_to_all | solution.py:331
  101.5 0.0 copy-start.1
  101.5 0.9 copy-done.1
  102.4 10.1 %shard_map.96 = (bf16[128,2048]{1,0:T(8,128)(2,1)}, bf16[768,16,128]{2,1,0:T(8,128)(2,1)}) custom-call(s32[128,128]{1,0:T(8,128)} %get-tuple-element.9.rows_ref, f32[128,4,128]{2,1,0:T(4,128)} %all_to_all.25.request_ref, bf16[128,3,8,128]{3,2,1,0:T(8,128)(2,1)} %copy-done.1, bf16[2048,2048]{1,0:T(8,128)(2,1)} %w_out_ref.1, bf16[1,2048]{1,0:T(2,128)(2,1)} %reshape.3.gain_ref), custom_call_target="tpu_custom_call" | custom-call | tf_op jit(solution)/shard_map/pallas_call | solution.py:369
  112.6 46.9 %all_to_all.26.x_ref = bf16[768,16,128]{2,1,0:T(8,128)(2,1)} all-to-all(bf16[768,16,128]{2,1,0:T(8,128)(2,1)} %get-tuple-element.12), channel_id=1, replica_groups=mesh['seq'=8,'grp'=16] {'seq','grp'}, dimensions={0} | all-to-all | bytes 6291456 | tf_op jit(solution)/shard_map/all_to_all | solution.py:331
  159.5 14.7 %shard_map.97 = bf16[768,16,128]{2,1,0:T(8,128)(2,1)} custom-call(s32[2]{0:T(128)} %pad_add_fusion.place_ref, s32[1,512]{1,0:T(1,128)} %get-tuple-element.11.slots_ref, bf16[768,16,128]{2,1,0:T(8,128)(2,1)} %all_to_all.26.x_ref, bf16[1,2048,768]{2,1,0:T(8,128)(2,1)} %gate_hbm.1, bf16[1,2048,768]{2,1,0:T(8,128)(2,1)} %up_hbm.1, ...), custom_call_target="tpu_custom_call" | custom-call | tf_op jit(solution)/shard_map/pallas_call | solution.py:384
  174.1 46.2 %all_to_all.27.x_ref = bf16[768,16,128]{2,1,0:T(8,128)(2,1)} all-to-all(bf16[768,16,128]{2,1,0:T(8,128)(2,1)} %shard_map.97), channel_id=1, replica_groups=mesh['seq'=8,'grp'=16] {'seq','grp'}, dimensions={0} | all-to-all | bytes 6291456 | tf_op jit(solution)/shard_map/all_to_all | solution.py:331
  220.3 6.8 %shard_map.98 = bf16[128,2048]{1,0:T(8,128)(2,1)} custom-call(s32[128,128]{1,0:T(8,128)} %get-tuple-element.9.rows_ref, bf16[128,2048]{1,0:T(8,128)(2,1)} %get-tuple-element.10.mixed_ref, bf16[768,16,128]{2,1,0:T(8,128)(2,1)} %all_to_all.27.x_ref), custom_call_target="tpu_custom_call" | custom-call | tf_op jit(solution)/shard_map/pallas_call | solution.py:399
Async XLA Ops:
  32.4 36.9 %all-to-all-start.1 = ((bf16[128,9,8,128]{3,2,1,0:T(8,128)(2,1)}), bf16[128,9,8,128]{3,2,1,0:T(8,128)(2,1)S(1)}, u32[]{:S(2)}, u32[]{:S(2)}) async-start(bf16[128,9,8,128]{3,2,1,0:T(8,128)(2,1)} %shard_map.94), calls=%async_computation.1 | async-start | bytes 4718592 | tf_op jit(solution)/shard_map/all_to_all | solution.py:331
  36.6 48.8 %copy-start.2 = (bf16[2048]{0:T(1024)(128)(2,1)S(1)}, bf16[2048]{0:T(1024)(128)(2,1)}, u32[]{:S(2)}) copy-start(bf16[2048]{0:T(1024)(128)(2,1)} %param.12) | copy-start | bytes 12292
  69.3 1.4 copy-start
  81.0 20.6 %all-to-all-start.2 = ((bf16[128,3,8,128]{3,2,1,0:T(8,128)(2,1)}), bf16[128,3,8,128]{3,2,1,0:T(8,128)(2,1)S(1)}, u32[]{:S(2)}, u32[]{:S(2)}) async-start(bf16[128,3,8,128]{3,2,1,0:T(8,128)(2,1)} %shard_map.95), calls=%async_computation.2 | async-start | bytes 1572864 | tf_op jit(solution)/shard_map/all_to_all | solution.py:331
  101.5 0.9 copy-start.1
where the time goes:
time: 228 us; the launch traced here: 227 us
  blocking collectives  116 us (51%)
  Pallas kernels  54.9 us (24%)
  waiting for transfers between devices  44 us (19%)
  starting transfers between devices  8.76 us (4%)
  local copies, waits for them, and re-layouts  2.92 us (1%)
    all_to_all x3, blocking collectives, exchange(): return lax.all_to_all(array, ALL, split_axis=0, concat_axis=0, tiled=True)  116 us
    all_to_all x2, waiting for transfers between devices, exchange(): return lax.all_to_all(array, ALL, split_axis=0, concat_axis=0, tiled=True)  44 us
    pallas_call x1, Pallas kernels, shards(): call(expert_kernel, shape((SENT, CHUNKS, 128)), [smem, smem, whole(), hbm...  14.7 us
    pallas_call x1, Pallas kernels, shards(): call(attend_kernel, shape((DEVICES, 3, 8, HEAD)), [whole(), whole()], [pl...  10.2 us
    pallas_call x1, Pallas kernels, shards(): call(mix_kernel, (shape((ROWS, WIDTH)), shape((SENT, CHUNKS, 128))), [sme...  10.1 us
    all_to_all x2, starting transfers between devices, exchange(): return lax.all_to_all(array, ALL, split_axis=0, concat_axis=0, tiled=True)  8.76 us
    pallas_call x1, Pallas kernels, shards(): pl.pallas_call(select_kernel, out_shape=shape((DEVICES, 9, 8, HEAD)), gri...  6.82 us
    pallas_call x1, Pallas kernels, shards(): call(combine_kernel, shape((ROWS, WIDTH)), [whole(), whole(), whole()], [...  6.81 us
  transfers between devices with their start and end apart: 2, of which 2 were waited for; matrix products, arithmetic and copies ran while one was open for 0% of the time, Pallas kernels for 2%

commit v1 on v0

v1 whole, which is shorter than its diff:
```python
import jax
import jax.numpy as jnp
from jax import lax
from jax.experimental import pallas as pl
from jax.experimental.pallas import tpu as pltpu
from jax.sharding import PartitionSpec as P

BF16 = jnp.bfloat16
F32 = jnp.float32
I32 = jnp.int32
ALL = ("seq", "grp")

SEQ = 8
GRP = 16
DEVICES = 128
ROWS = 128
HEAD = 128
WIDTH = 2048
CHUNKS = WIDTH // 128
CLUSTER = 1024
SLOTS = 12
LOW = 8
HIGH = 4
ESLOTS = 6
CHOSEN = 512
HIDDEN = 768
SENT = DEVICES * ESLOTS
GROUP = 32
FAR = -1e30
GROWS = GROUP * SLOTS
PLACES = DEVICES * SLOTS

NN = (((1,), (0,)), ((), ()))
NT = (((1,), (1,)), ((), ()))
TN = (((0,), (0,)), ((), ()))
VMEM_LIMIT = 60 * 1024 * 1024


def iota(shape, axis):
    return lax.broadcasted_iota(I32, shape, axis)


def dot(a, b, dims=NN):
    return lax.dot_general(a, b, dims, preferred_element_type=F32)


def whole(space=pltpu.VMEM):
    return pl.BlockSpec(memory_space=space)


def rank_in_block(block, most):
    lane = iota(block.shape, 1)
    rank = jnp.zeros(block.shape, I32)
    for back in range(1, most):
        same = (pltpu.roll(block, back, 1) == block) & (lane >= back)
        rank = rank + jnp.where(same, 1, 0)
    return rank


def request_kernel(lists_ref, out_ref):
    line = iota((128, CLUSTER), 0)
    asked = jnp.zeros((DEVICES, 128), F32)
    for h in range(2):
        token = lists_ref[h]
        block = token >> 7
        slot_line = h * 16 + rank_in_block(block, SLOTS)
        row = ((token & 127) + 1).astype(F32)
        member = jnp.where(block == line, 1.0, 0.0).astype(BF16)
        rows = jnp.where(slot_line == line, row, 0.0).astype(BF16)
        asked = asked + dot(member, rows, NT)
    out_ref[...] = asked


def place_order(index):
    group = index // GROWS
    inner = index - group * GROWS
    upper = inner - GROUP * LOW
    is_low = inner < GROUP * LOW
    source = group * GROUP + jnp.where(is_low, inner >> 3, upper >> 2)
    slot = jnp.where(is_low, inner & 7, LOW + (upper & 3))
    return source, slot


def empty_kernel(lists_ref, out_ref):
    line = iota((128, CLUSTER), 0)
    source, slot = place_order(iota((PLACES, 128), 0))
    lane = iota((PLACES, 128), 1)
    spread = jnp.where(lane == source, 1.0, 0.0).astype(BF16)
    for h in range(2):
        member = jnp.where((lists_ref[h] >> 7) == line, 1.0, 0.0).astype(BF16)
        count = dot(member, jnp.ones((CLUSTER, 128), BF16)).astype(BF16)
        held = dot(spread, count)
        empty = (slot.astype(F32) >= held) & (lane == 0)
        out_ref[h] = jnp.where(empty, FAR, 0.0).astype(BF16)


def expert_index_kernel(place_ref, lists_ref, marks_ref, rows_ref, slots_ref):
    me = place_ref[0]
    lists = lists_ref[...]
    inside = (lists >> 7) == me
    position = iota((DEVICES, CHOSEN), 1)
    before = jnp.sum(jnp.where(lists < me * ROWS, 1.0, 0.0), axis=1, keepdims=True).astype(I32)
    row = (lists - me * ROWS + 1).astype(F32)
    rank = jnp.where(inside, position - before, -1)
    lane = iota((DEVICES, 128), 1)
    rows = jnp.zeros((DEVICES, 128), F32)
    for k in range(ESLOTS):
        found = jnp.sum(jnp.where(rank == k, row, 0.0), axis=1, keepdims=True)
        rows = jnp.where(lane == k, found, rows)
    marks = rows.T[:8].astype(I32)
    marks_ref[...] = marks
    rows_ref[...] = jnp.maximum(marks - 1, 0)
    mine = lists_ref[pl.ds(me, 1), :]
    block = mine >> 7
    slots_ref[...] = block * ESLOTS + rank_in_block(block, ESLOTS)


def wanted_rows(asked):
    asked = asked.astype(BF16)
    line = iota((128, 128), 0)
    lane = iota((128, 128), 1)
    seq_of = jnp.where(iota((SEQ, 128), 1) >> 4 == iota((SEQ, 128), 0), 1.0, 0.0).astype(BF16)
    wanted = []
    for kind in range(3):
        slot = (lane & 7) + 16 * kind if kind < 2 else ((lane >> 2) & 1) * 16 + LOW + (lane & 3)
        placed = dot(asked, jnp.where(line == slot, 1.0, 0.0).astype(BF16))
        placed = jnp.where((line & 15) == lane >> 3, placed, 0.0).astype(BF16)
        wanted.append(dot(seq_of, placed))
    return wanted


def select_kernel(asked_ref, qkv_ref, wanted_ref, out_ref):
    wanted = wanted_rows(asked_ref[...])
    for kind in range(3):
        wanted_ref[kind] = wanted[kind]
    token = (iota((ROWS, 128), 0) + 1).astype(F32)
    lane_head = (iota((ROWS, 128), 1) >> 2) & 1
    for s in range(SEQ):
        peers = slice(s * GRP, (s + 1) * GRP)
        high_match = wanted[2][s : s + 1, :] == token
        high = jnp.zeros((128, 3 * HEAD), F32)
        for h in range(2):
            start = (2 * s + h) * HEAD
            packed = jnp.concatenate(
                [qkv_ref[c, :, start : start + HEAD] for c in range(3)], axis=1
            )
            low_match = jnp.where(wanted[h][s : s + 1, :] == token, 1.0, 0.0).astype(BF16)
            low = dot(low_match, packed, TN).astype(BF16)
            mine = jnp.where(high_match & (lane_head == h), 1.0, 0.0).astype(BF16)
            high = high + dot(mine, packed, TN)
            for c in range(3):
                out_ref[peers, h * 3 + c] = low[:, c * HEAD : (c + 1) * HEAD].reshape(GRP, 8, HEAD)
        high = high.astype(BF16)
        for c in range(3):
            out_ref[peers, 6 + c] = high[:, c * HEAD : (c + 1) * HEAD].reshape(GRP, 8, HEAD)


def attend_kernel(empty_ref, x_ref, out_ref, packed_ref, causal_ref):
    factor = HEAD ** (-0.5) * 1.4426950408889634
    low_rows = GROUP * LOW
    high_rows = GROUP * HIGH
    joint = iota((2 * high_rows, high_rows), 0)
    apart = iota((2 * high_rows, high_rows), 1)
    same_place = (joint >> 3) * HIGH + (joint & 3) == apart
    spread = [
        jnp.where(same_place & (((joint >> 2) & 1) == h), 1.0, 0.0).astype(BF16) for h in range(2)
    ]

    def order_of(index):
        source, slot = place_order(index)
        return source * SLOTS + slot

    later = order_of(iota((1, GROWS), 1)) > order_of(iota((GROWS, 1), 0))
    causal_ref[...] = jnp.where(later, FAR, 0.0)
    first_lane = jnp.where(iota((GROWS, 128), 1) == 0, 1.0, 0.0).astype(BF16)
    for i in range(DEVICES // GROUP):
        blocks = slice(i * GROUP, (i + 1) * GROUP)
        start, stop = i * GROWS, (i + 1) * GROWS
        for c in range(3):
            both = x_ref[blocks, 6 + c].reshape(2 * high_rows, HEAD)
            for h in range(2):
                packed_ref[h, c, start : start + low_rows, :] = x_ref[blocks, h * 3 + c].reshape(
                    low_rows, HEAD
                )
                packed_ref[h, c, start + low_rows : stop, :] = dot(spread[h], both, TN).astype(BF16)
        joined = jnp.zeros((2 * high_rows, HEAD), F32)
        for h in range(2):

            def keys(begin, end):
                return jnp.concatenate(
                    [packed_ref[h, 1, begin:end, :], empty_ref[h, begin:end, :]], axis=1
                )

            def values(begin, end):
                return jnp.concatenate(
                    [packed_ref[h, 2, begin:end, :], jnp.ones((end - begin, 128), BF16)], axis=1
                )

            queries = jnp.concatenate([packed_ref[h, 0, start:stop, :], first_lane], axis=1)
            near = dot(queries, keys(start, stop), NT) + causal_ref[...]
            top = jnp.max(near, axis=1, keepdims=True)
            if i:
                far = dot(queries, keys(0, start), NT)
                top = jnp.maximum(top, jnp.max(far, axis=1, keepdims=True))
            near = jnp.exp2((near - top) * factor).astype(BF16)
            summed = dot(near, values(start, stop))
            if i:
                far = jnp.exp2((far - top) * factor).astype(BF16)
                summed = summed + dot(far, values(0, start))
            result = (summed[:, :HEAD] / summed[:, HEAD:]).astype(BF16)
            out_ref[blocks, h] = result[:low_rows].reshape(GROUP, 8, HEAD)
            joined = joined + dot(spread[h], result[low_rows:])
        out_ref[blocks, 2] = joined.astype(BF16).reshape(GROUP, 8, HEAD)


def mix_kernel(
    rows_ref, wanted_ref, came_ref, w_out_ref, gain_ref, mixed_ref, out_hbm,
    w_ref, att_ref, tall_ref, tile_ref, out_ref, w_sems, out_sems,
):
    parts = w_sems.shape[0]
    depth = WIDTH // parts
    copies = [
        pltpu.make_async_copy(
            w_out_ref.at[pl.ds(p * depth, depth), :], w_ref.at[pl.ds(p * depth, depth), :], w_sems.at[p]
        )
        for p in range(parts)
    ]
    for copy in copies:
        copy.start()
    token = (iota((ROWS, 128), 0) + 1).astype(F32)
    lane_head = (iota((ROWS, 128), 1) >> 2) & 1
    for s in range(SEQ):
        peers = slice(s * GRP, (s + 1) * GRP)
        high_match = wanted_ref[2, s : s + 1, :] == token
        high = came_ref[peers, 2].reshape(128, HEAD)
        for h in range(2):
            low_match = jnp.where(wanted_ref[h, s : s + 1, :] == token, 1.0, 0.0).astype(BF16)
            mine = jnp.where(high_match & (lane_head == h), 1.0, 0.0).astype(BF16)
            got = dot(
                jnp.concatenate([low_match, mine], axis=1),
                jnp.concatenate([came_ref[peers, h].reshape(128, HEAD), high], axis=0),
            )
            start = (2 * s + h) * HEAD
            att_ref[:, start : start + HEAD] = got.astype(BF16)
    total = jnp.zeros((ROWS, WIDTH), F32)
    for p in range(parts):
        copies[p].wait()
        total = total + dot(
            att_ref[:, p * depth : (p + 1) * depth], w_ref[p * depth : (p + 1) * depth, :]
        )
    mixed = total.astype(BF16)
    mixed_ref[...] = mixed
    wide = mixed.astype(F32)
    mean_square = jnp.mean(wide * wide, axis=1, keepdims=True)
    normed = wide * lax.rsqrt(mean_square + 1e-06) * gain_ref[...].astype(F32)
    for j in range(CHUNKS):
        tall_ref[pl.ds(j, ROWS, stride=CHUNKS), :] = normed[:, j * 128 : (j + 1) * 128]
    tile_ref[...] = tall_ref[...].astype(BF16).reshape(ROWS, CHUNKS, 128)
    sends = out_sems.shape[0]
    share = DEVICES // sends
    outs = []
    for p in range(sends):
        for e in range(p * share, (p + 1) * share):
            for k in range(ESLOTS):
                out_ref[e * ESLOTS + k] = tile_ref[rows_ref[k, e]]
        span = pl.ds(p * share * ESLOTS, share * ESLOTS)
        outs.append(pltpu.make_async_copy(out_ref.at[span], out_hbm.at[span], out_sems.at[p]))
        outs[-1].start()
    for copy in outs:
        copy.wait()


def expert_kernel(
    place_ref, slots_ref, x_ref, gate_hbm, up_hbm, down_hbm, router_ref, out_ref,
    gate_ref, up_ref, down_ref, tall_ref, rows_ref, hidden_ref, back_ref, sems,
):
    copies = [
        pltpu.make_async_copy(source.at[0], target, sems.at[n])
        for n, (source, target) in enumerate(
            [(gate_hbm, gate_ref), (up_hbm, up_ref), (down_hbm, down_ref)]
        )
    ]
    for copy in copies:
        copy.start()
    parts, half = rows_ref.shape[:2]
    me = place_ref[0]

    def take(part, begin, end):
        for i in range(begin, end):
            tall_ref[part, i * CHUNKS : (i + 1) * CHUNKS, :] = x_ref[
                slots_ref[0, part * half + i]
            ].astype(F32)

    def flatten(part, begin, end):
        for j in range(begin, end):
            rows_ref[part, :, j * 128 : (j + 1) * 128] = tall_ref[
                part, pl.ds(j, half, stride=CHUNKS), :
            ].astype(BF16)

    def put(part, begin, end):
        for i in range(begin, end):
            out_ref[slots_ref[0, part * half + i]] = back_ref[
                part, i * CHUNKS : (i + 1) * CHUNKS, :
            ].astype(BF16)

    take(0, 0, half)
    flatten(0, 0, CHUNKS)
    wide = HIDDEN // 3
    for part in range(parts):
        for n in range(3):
            columns = slice(n * wide, (n + 1) * wide)
            if part == 0 and n == 0:
                copies[0].wait()
            gate = dot(rows_ref[part], gate_ref[:, columns])
            if part == 0 and n == 0:
                copies[1].wait()
            up = dot(rows_ref[part], up_ref[:, columns])
            if part == 0:
                if n < 2:
                    out_ref[n * SENT // 2 : (n + 1) * SENT // 2] = jnp.zeros(
                        (SENT // 2, CHUNKS, 128), BF16
                    )
                    take(1, n * half // 2, (n + 1) * half // 2)
                else:
                    flatten(1, 0, CHUNKS)
            else:
                put(0, n * half // 3, (n + 1) * half // 3)
            hidden_ref[part, :, columns] = (jax.nn.silu(gate) * up).astype(BF16)
        logits = dot(rows_ref[part], router_ref[...])
        mine = jnp.where(iota((half, 128), 1) == me, logits, 0.0)
        weight = jax.nn.sigmoid(jnp.sum(mine, axis=1, keepdims=True))
        if part == 0:
            copies[2].wait()
        for n in range(4):
            result = dot(hidden_ref[part], down_ref[:, n * 512 : (n + 1) * 512]) * weight
            for j in range(4):
                back_ref[part, pl.ds(4 * n + j, half, stride=CHUNKS), :] = result[
                    :, j * 128 : (j + 1) * 128
                ]
    put(1, 0, half)


def combine_kernel(marks_ref, mixed_ref, x_ref, out_ref, tall_ref):
    for e in range(DEVICES):
        for k in range(ESLOTS):
            start = (k * DEVICES + e) * CHUNKS
            tall_ref[start : start + CHUNKS, :] = x_ref[e * ESLOTS + k].astype(F32)
    token = iota((ROWS, DEVICES), 0) + 1
    match = jnp.concatenate(
        [jnp.where(marks_ref[k : k + 1, :] == token, 1.0, 0.0) for k in range(ESLOTS)], axis=1
    ).astype(BF16)
    for n in range(CHUNKS // 2):
        flat = jnp.concatenate(
            [
                tall_ref[pl.ds(2 * n + j, SENT, stride=CHUNKS), :].astype(BF16)
                for j in range(2)
            ],
            axis=1,
        )
        columns = slice(n * 256, (n + 1) * 256)
        out_ref[:, columns] = (mixed_ref[:, columns].astype(F32) + dot(match, flat)).astype(BF16)


def call(kernel, out_shape, in_specs, scratch=(), out_specs=None):
    return pl.pallas_call(
        kernel,
        out_shape=out_shape,
        in_specs=in_specs,
        out_specs=jax.tree.map(lambda _: whole(), out_shape) if out_specs is None else out_specs,
        scratch_shapes=list(scratch),
        compiler_params=pltpu.CompilerParams(vmem_limit_bytes=VMEM_LIMIT),
    )


def shape(dims, dtype=BF16):
    return jax.ShapeDtypeStruct(dims, dtype)


def exchange(array):
    return lax.all_to_all(array, ALL, split_axis=0, concat_axis=0, tiled=True)


def near(array):
    return pltpu.with_memory_space_constraint(array, pltpu.VMEM)


def shards(qkv, cluster_lists, w_out, norm_gain, router, expert_lists, w_gate, w_up, w_down):
    me = lax.axis_index("seq") * GRP + lax.axis_index("grp")
    place = me.reshape(1).astype(I32)
    smem = whole(pltpu.SMEM)
    hbm = whole(pl.ANY)

    request = call(request_kernel, shape((DEVICES, 128), F32), [whole()])(cluster_lists)
    asked = exchange(request.reshape(DEVICES, 1, 128)).reshape(DEVICES, 128)
    empty = call(empty_kernel, shape((2, PLACES, 128)), [whole()])(cluster_lists)
    marks, rows, slots = call(
        expert_index_kernel,
        (shape((8, DEVICES), I32), shape((8, DEVICES), I32), shape((1, CHOSEN), I32)),
        [smem, whole()],
    )(place, expert_lists)

    wanted, picked = call(
        select_kernel,
        (shape((3, SEQ, 128), F32), shape((DEVICES, 9, 8, HEAD))),
        [whole(), whole()],
    )(asked, near(qkv.transpose(1, 0, 2)))
    arrived = exchange(picked)

    outputs = call(
        attend_kernel,
        shape((DEVICES, 3, 8, HEAD)),
        [whole(), whole()],
        [pltpu.VMEM((2, 3, PLACES, HEAD), BF16), pltpu.VMEM((GROWS, GROWS), F32)],
    )(empty, near(arrived))
    came_back = exchange(outputs)

    mixed, outgoing = call(
        mix_kernel,
        (shape((ROWS, WIDTH)), shape((SENT, CHUNKS, 128))),
        [smem, whole(), whole(), hbm, whole()],
        [
            pltpu.VMEM((WIDTH, WIDTH), BF16),
            pltpu.VMEM((ROWS, WIDTH), BF16),
            pltpu.VMEM((ROWS * CHUNKS, 128), F32),
            pltpu.VMEM((ROWS, CHUNKS, 128), BF16),
            pltpu.VMEM((SENT, CHUNKS, 128), BF16),
            pltpu.SemaphoreType.DMA((4,)),
            pltpu.SemaphoreType.DMA((4,)),
        ],
        out_specs=(whole(), hbm),
    )(rows, wanted, near(came_back), w_out, norm_gain.reshape(1, WIDTH))
    incoming = exchange(outgoing)

    half = CHOSEN // 2
    produced = call(
        expert_kernel,
        shape((SENT, CHUNKS, 128)),
        [smem, smem, whole(), hbm, hbm, hbm, whole()],
        [
            pltpu.VMEM((WIDTH, HIDDEN), BF16),
            pltpu.VMEM((WIDTH, HIDDEN), BF16),
            pltpu.VMEM((HIDDEN, WIDTH), BF16),
            pltpu.VMEM((2, half * CHUNKS, 128), F32),
            pltpu.VMEM((2, half, WIDTH), BF16),
            pltpu.VMEM((2, half, HIDDEN), BF16),
            pltpu.VMEM((2, half * CHUNKS, 128), F32),
            pltpu.SemaphoreType.DMA((3,)),
        ],
    )(place, slots, incoming, w_gate, w_up, w_down, router)
    results = exchange(produced)

    return call(
        combine_kernel,
        shape((ROWS, WIDTH)),
        [whole(), whole(), whole()],
        [pltpu.VMEM((SENT * CHUNKS, 128), F32)],
    )(marks, mixed, results)


def solution(mesh):
    return jax.shard_map(
        shards,
        mesh=mesh,
        in_specs=(
            P(("seq", "grp"), None, None),
            P("seq", "grp", None),
            P(),
            P(),
            P(),
            P(),
            P(("seq", "grp"), None, None),
            P(("seq", "grp"), None, None),
            P(("seq", "grp"), None, None),
        ),
        out_specs=P(("seq", "grp"), None),
        check_vma=False,
    )
```

time: 228 us -> 217 us (0.952)
  Pallas kernels: 54.9 us -> 47.5 us
    pallas_call x4, Pallas kernels: 13.1 us -> 9.87 us  [the longest x1 3.56 us: shards(): call(select_kernel, (shape((3, SEQ, 128), F32), shape((DEVICES, 9, 8, HEA...]
where the time goes in v1:
time: 217 us
  blocking collectives  114 us (53%)
  Pallas kernels  47.5 us (22%)
  waiting for transfers between devices  43.6 us (20%)
  starting transfers between devices  9.07 us (4%)
    all_to_all x3, blocking collectives, exchange(): return lax.all_to_all(array, ALL, split_axis=0, concat_axis=0, tiled=True)  114 us
    all_to_all x2, waiting for transfers between devices, exchange(): return lax.all_to_all(array, ALL, split_axis=0, concat_axis=0, tiled=True)  43.6 us
    pallas_call x1, Pallas kernels, shards(): call(expert_kernel, shape((SENT, CHUNKS, 128)), [smem, smem, whole(), hbm...  14.9 us
    pallas_call x1, Pallas kernels, shards(): call(attend_kernel, shape((DEVICES, 3, 8, HEAD)), [whole(), whole()], [pl...  9.41 us
    all_to_all x2, starting transfers between devices, exchange(): return lax.all_to_all(array, ALL, split_axis=0, concat_axis=0, tiled=True)  9.07 us
    pallas_call x1, Pallas kernels, shards(): call(mix_kernel, (shape((ROWS, WIDTH)), shape((SENT, CHUNKS, 128))), [sme...  7.98 us
    pallas_call x1, Pallas kernels, shards(): call(combine_kernel, shape((ROWS, WIDTH)), [whole(), whole(), whole()], [...  5.36 us
  transfers between devices with their start and end apart: 2, of which 2 were waited for; matrix products, arithmetic and copies ran while one was open for 0% of the time, Pallas kernels for 2%

profile of v1, /device:TPU:1, one launch (start us, length us, event | category | flops | bytes accessed | tf_op | source)
XLA Modules:
  0.0 216.7 jit_solution(10353815481580210206)
XLA Ops:
  0.0 1.9 shard_map.92
  1.9 21.4 %all_to_all.25 = f32[128,1,128]{2,1,0:T(1,128)} all-to-all(f32[128,1,128]{2,1,0:T(1,128)} %bitcast.8), channel_id=1, replica_groups=mesh['seq'=8,'grp'=16] {'seq','grp'}, dimensions={0} | all-to-all | bytes 131072 | tf_op jit(solution)/shard_map/all_to_all | solution.py:380
  23.3 0.0 copy-start
  23.3 1.4 copy-done
  24.7 3.6 %shard_map.93 = (f32[3,8,128]{2,1,0:T(8,128)}, bf16[128,9,8,128]{3,2,1,0:T(8,128)(2,1)}) custom-call(f32[128,128]{1,0:T(8,128)} %bitcast.7, bf16[3,128,2048]{2,1,0:T(8,128)(2,1)S(1)} %bitcast.6), custom_call_target="tpu_custom_call" | custom-call | tf_op jit(solution)/shard_map/pallas_call | solution.py:402
  28.3 4.6 %all-to-all-start.1 = ((bf16[128,9,8,128]{3,2,1,0:T(8,128)(2,1)}), bf16[128,9,8,128]{3,2,1,0:T(8,128)(2,1)S(1)}, u32[]{:S(2)}, u32[]{:S(2)}) async-start(bf16[128,9,8,128]{3,2,1,0:T(8,128)(2,1)} %get-tuple-element.15), calls=%async_computation.1 | async-start | bytes 4718592 | tf_op jit(solution)/shard_map/all_to_all | solution.py:380
  32.8 0.0 copy-start.1
  32.9 2.5 %shard_map.94.empty_ref = bf16[2,1536,128]{2,1,0:T(8,128)(2,1)} custom-call(s32[2,1,1024]{2,1,0:T(1,128)} %lists_ref.5), custom_call_target="tpu_custom_call" | custom-call | tf_op jit(solution)/shard_map/pallas_call | solution.py:395
  35.4 30.0 %all-to-all-done.1.x_ref = bf16[128,9,8,128]{3,2,1,0:T(8,128)(2,1)S(1)} async-done(((bf16[128,9,8,128]{3,2,1,0:T(8,128)(2,1)}), bf16[128,9,8,128]{3,2,1,0:T(8,128)(2,1)S(1)}, u32[]{:S(2)}, u32[]{:S(2)}) %all-to-all-start.1) | async-done | bytes 2359328 | tf_op jit(solution)/shard_map/all_to_all | solution.py:380
  65.4 9.4 %shard_map.95 = bf16[128,3,8,128]{3,2,1,0:T(8,128)(2,1)} custom-call(bf16[2,1536,128]{2,1,0:T(8,128)(2,1)} %shard_map.94.empty_ref, bf16[128,9,8,128]{3,2,1,0:T(8,128)(2,1)S(1)} %all-to-all-done.1.x_ref), custom_call_target="tpu_custom_call" | custom-call | tf_op jit(solution)/shard_map/pallas_call | solution.py:409
  74.8 4.5 %all-to-all-start.2 = ((bf16[128,3,8,128]{3,2,1,0:T(8,128)(2,1)}), bf16[128,3,8,128]{3,2,1,0:T(8,128)(2,1)S(1)}, u32[]{:S(2)}, u32[]{:S(2)}) async-start(bf16[128,3,8,128]{3,2,1,0:T(8,128)(2,1)} %shard_map.95), calls=%async_computation.2 | async-start | bytes 1572864 | tf_op jit(solution)/shard_map/all_to_all | solution.py:380
  79.3 0.0 copy-done.1
  79.3 0.6 reshape.15.gain_ref
  79.9 1.9 shard_map.91
  81.8 13.5 %all-to-all-done.2.came_ref = bf16[128,3,8,128]{3,2,1,0:T(8,128)(2,1)S(1)} async-done(((bf16[128,3,8,128]{3,2,1,0:T(8,128)(2,1)}), bf16[128,3,8,128]{3,2,1,0:T(8,128)(2,1)S(1)}, u32[]{:S(2)}, u32[]{:S(2)}) %all-to-all-start.2) | async-done | bytes 786464 | tf_op jit(solution)/shard_map/all_to_all | solution.py:380
  95.4 8.0 %shard_map.96 = (bf16[128,2048]{1,0:T(8,128)(2,1)}, bf16[768,16,128]{2,1,0:T(8,128)(2,1)}) custom-call(s32[8,128]{1,0:T(8,128)} %get-tuple-element.13.rows_ref, f32[3,8,128]{2,1,0:T(8,128)} %get-tuple-element.14.wanted_ref, bf16[128,3,8,128]{3,2,1,0:T(8,128)(2,1)S(1)} %all-to-all-done.2.came_ref, bf16[2048,2048]{1,0:T(8,128)(2,1)} %w_out_ref.1, ...), custom_call_target="tpu_custom_call" | custom-call | tf_op jit(solution)/shard_map/pallas_call | solution.py:417
  103.4 46.9 %all_to_all.26.x_ref = bf16[768,16,128]{2,1,0:T(8,128)(2,1)} all-to-all(bf16[768,16,128]{2,1,0:T(8,128)(2,1)} %get-tuple-element.18), channel_id=1, replica_groups=mesh['seq'=8,'grp'=16] {'seq','grp'}, dimensions={0} | all-to-all | bytes 6291456 | tf_op jit(solution)/shard_map/all_to_all | solution.py:380
  150.3 14.9 %shard_map.97 = bf16[768,16,128]{2,1,0:T(8,128)(2,1)} custom-call(s32[1]{0:T(128)} %bitcast.place_ref, s32[1,512]{1,0:T(1,128)} %get-tuple-element.17.slots_ref, bf16[768,16,128]{2,1,0:T(8,128)(2,1)} %all_to_all.26.x_ref, bf16[1,2048,768]{2,1,0:T(8,128)(2,1)} %gate_hbm.1, bf16[1,2048,768]{2,1,0:T(8,128)(2,1)} %up_hbm.1, bf16[1,768,2048]{2,1,0:T(8,128)(2,1)} %down_hbm.1, ...), custom_call_target="tpu_custom_call" | custom-call | tf_op jit(solution)/shard_map/pallas_call | solution.py:435
  165.1 46.2 %all_to_all.27.x_ref = bf16[768,16,128]{2,1,0:T(8,128)(2,1)} all-to-all(bf16[768,16,128]{2,1,0:T(8,128)(2,1)} %shard_map.97), channel_id=1, replica_groups=mesh['seq'=8,'grp'=16] {'seq','grp'}, dimensions={0} | all-to-all | bytes 6291456 | tf_op jit(solution)/shard_map/all_to_all | solution.py:380
  211.3 5.4 %shard_map.98 = bf16[128,2048]{1,0:T(8,128)(2,1)} custom-call(s32[8,128]{1,0:T(8,128)} %get-tuple-element.12.marks_ref, bf16[128,2048]{1,0:T(8,128)(2,1)} %get-tuple-element.16.mixed_ref, bf16[768,16,128]{2,1,0:T(8,128)(2,1)} %all_to_all.27.x_ref), custom_call_target="tpu_custom_call" | custom-call | tf_op jit(solution)/shard_map/pallas_call | solution.py:452
Async XLA Ops:
  23.3 1.4 copy-start
  28.3 37.1 %all-to-all-start.1 = ((bf16[128,9,8,128]{3,2,1,0:T(8,128)(2,1)}), bf16[128,9,8,128]{3,2,1,0:T(8,128)(2,1)S(1)}, u32[]{:S(2)}, u32[]{:S(2)}) async-start(bf16[128,9,8,128]{3,2,1,0:T(8,128)(2,1)} %get-tuple-element.15), calls=%async_computation.1 | async-start | bytes 4718592 | tf_op jit(solution)/shard_map/all_to_all | solution.py:380
  32.8 46.5 %copy-start.1 = (bf16[2048]{0:T(1024)(128)(2,1)S(1)}, bf16[2048]{0:T(1024)(128)(2,1)}, u32[]{:S(2)}) copy-start(bf16[2048]{0:T(1024)(128)(2,1)} %param.12) | copy-start | bytes 12292
  74.8 20.6 %all-to-all-start.2 = ((bf16[128,3,8,128]{3,2,1,0:T(8,128)(2,1)}), bf16[128,3,8,128]{3,2,1,0:T(8,128)(2,1)S(1)}, u32[]{:S(2)}, u32[]{:S(2)}) async-start(bf16[128,3,8,128]{3,2,1,0:T(8,128)(2,1)} %shard_map.95), calls=%async_computation.2 | async-start | bytes 1572864 | tf_op jit(solution)/shard_map/all_to_all | solution.py:380

commit v2 on v1

--- a/solution.py
+++ b/solution.py
@@ -27,6 +27,8 @@
 SENT = DEVICES * ESLOTS
 GROUP = 32
 FAR = -1e30
+PIECES = 3
+PITCH = CHUNKS + 1
 GROWS = GROUP * SLOTS
 PLACES = DEVICES * SLOTS
 
@@ -83,15 +85,13 @@
 
 def empty_kernel(lists_ref, out_ref):
     line = iota((128, CLUSTER), 0)
-    source, slot = place_order(iota((PLACES, 128), 0))
-    lane = iota((PLACES, 128), 1)
-    spread = jnp.where(lane == source, 1.0, 0.0).astype(BF16)
+    source, slot = place_order(iota((1, PLACES), 1))
+    spread = jnp.where(iota((128, PLACES), 0) == source, 1.0, 0.0).astype(BF16)
     for h in range(2):
         member = jnp.where((lists_ref[h] >> 7) == line, 1.0, 0.0).astype(BF16)
-        count = dot(member, jnp.ones((CLUSTER, 128), BF16)).astype(BF16)
-        held = dot(spread, count)
-        empty = (slot.astype(F32) >= held) & (lane == 0)
-        out_ref[h] = jnp.where(empty, FAR, 0.0).astype(BF16)
+        count = dot(jnp.ones((8, CLUSTER), BF16), member, NT)
+        held = dot(count.astype(BF16), spread)
+        out_ref[h] = jnp.where(slot.astype(F32) < held, 0.0, FAR)
 
 
 def expert_index_kernel(place_ref, lists_ref, marks_ref, rows_ref, slots_ref):
@@ -155,7 +155,7 @@
             out_ref[peers, 6 + c] = high[:, c * HEAD : (c + 1) * HEAD].reshape(GRP, 8, HEAD)
 
 
-def attend_kernel(empty_ref, x_ref, out_ref, packed_ref, causal_ref):
+def attend_kernel(empty_ref, x_ref, out_ref, packed_ref, causal_ref, result_ref):
     factor = HEAD ** (-0.5) * 1.4426950408889634
     low_rows = GROUP * LOW
     high_rows = GROUP * HIGH
@@ -172,8 +172,8 @@
 
     later = order_of(iota((1, GROWS), 1)) > order_of(iota((GROWS, 1), 0))
     causal_ref[...] = jnp.where(later, FAR, 0.0)
-    first_lane = jnp.where(iota((GROWS, 128), 1) == 0, 1.0, 0.0).astype(BF16)
-    for i in range(DEVICES // GROUP):
+    groups = DEVICES // GROUP
+    for i in range(groups):
         blocks = slice(i * GROUP, (i + 1) * GROUP)
         start, stop = i * GROWS, (i + 1) * GROWS
         for c in range(3):
@@ -183,34 +183,50 @@
                     low_rows, HEAD
                 )
                 packed_ref[h, c, start + low_rows : stop, :] = dot(spread[h], both, TN).astype(BF16)
-        joined = jnp.zeros((2 * high_rows, HEAD), F32)
-        for h in range(2):
-
-            def keys(begin, end):
-                return jnp.concatenate(
-                    [packed_ref[h, 1, begin:end, :], empty_ref[h, begin:end, :]], axis=1
-                )
-
-            def values(begin, end):
-                return jnp.concatenate(
-                    [packed_ref[h, 2, begin:end, :], jnp.ones((end - begin, 128), BF16)], axis=1
-                )
-
-            queries = jnp.concatenate([packed_ref[h, 0, start:stop, :], first_lane], axis=1)
-            near = dot(queries, keys(start, stop), NT) + causal_ref[...]
-            top = jnp.max(near, axis=1, keepdims=True)
-            if i:
-                far = dot(queries, keys(0, start), NT)
-                top = jnp.maximum(top, jnp.max(far, axis=1, keepdims=True))
-            near = jnp.exp2((near - top) * factor).astype(BF16)
-            summed = dot(near, values(start, stop))
-            if i:
-                far = jnp.exp2((far - top) * factor).astype(BF16)
-                summed = summed + dot(far, values(0, start))
-            result = (summed[:, :HEAD] / summed[:, HEAD:]).astype(BF16)
-            out_ref[blocks, h] = result[:low_rows].reshape(GROUP, 8, HEAD)
-            joined = joined + dot(spread[h], result[low_rows:])
-        out_ref[blocks, 2] = joined.astype(BF16).reshape(GROUP, 8, HEAD)
+
+    piece = GROWS // PIECES
+
+    def score(i, h, q):
+        start, stop = i * GROWS, (i + 1) * GROWS
+        inner = slice(q * piece, (q + 1) * piece)
+        queries = packed_ref[h, 0, start + q * piece : start + (q + 1) * piece, :]
+        near = dot(queries, packed_ref[h, 1, start:stop, :], NT)
+        near = near + causal_ref[inner, :] + empty_ref[h, 0:1, start:stop]
+        if i == 0:
+            return (near,)
+        far = dot(queries, packed_ref[h, 1, :start, :], NT) + empty_ref[h, 0:1, :start]
+        return (near, far)
+
+    def finish(i, h, q, scores):
+        start, stop = i * GROWS, (i + 1) * GROWS
+        top = jnp.max(scores[0], axis=1, keepdims=True)
+        for part in scores[1:]:
+            top = jnp.maximum(top, jnp.max(part, axis=1, keepdims=True))
+        summed = jnp.zeros((piece, 2 * HEAD), F32)
+        for part, (begin, end) in zip(scores, ((start, stop), (0, start))):
+            weights = jnp.exp2((part - top) * factor).astype(BF16)
+            values = jnp.concatenate(
+                [packed_ref[h, 2, begin:end, :], jnp.ones((end - begin, 128), BF16)], axis=1
+            )
+            summed = summed + dot(weights, values)
+        result_ref[q * piece : (q + 1) * piece, :] = (summed[:, :HEAD] / summed[:, HEAD:]).astype(BF16)
+
+    steps = [(i, h, q) for i in range(groups) for h in range(2) for q in range(PIECES)]
+    ready = score(*steps[0])
+    joined = None
+    for n, (i, h, q) in enumerate(steps):
+        scores = ready
+        if n + 1 < len(steps):
+            ready = score(*steps[n + 1])
+        finish(i, h, q, scores)
+        if q < PIECES - 1:
+            continue
+        blocks = slice(i * GROUP, (i + 1) * GROUP)
+        out_ref[blocks, h] = result_ref[:low_rows].reshape(GROUP, 8, HEAD)
+        part = dot(spread[h], result_ref[low_rows:])
+        joined = part if h == 0 else joined + part
+        if h == 1:
+            out_ref[blocks, 2] = joined.astype(BF16).reshape(GROUP, 8, HEAD)
 
 
 def mix_kernel(
@@ -218,11 +234,9 @@
     w_ref, att_ref, tall_ref, tile_ref, out_ref, w_sems, out_sems,
 ):
     parts = w_sems.shape[0]
-    depth = WIDTH // parts
+    span = WIDTH // parts
     copies = [
-        pltpu.make_async_copy(
-            w_out_ref.at[pl.ds(p * depth, depth), :], w_ref.at[pl.ds(p * depth, depth), :], w_sems.at[p]
-        )
+        pltpu.make_async_copy(w_out_ref.at[:, pl.ds(p * span, span)], w_ref.at[p], w_sems.at[p])
         for p in range(parts)
     ]
     for copy in copies:
@@ -242,20 +256,17 @@
             )
             start = (2 * s + h) * HEAD
             att_ref[:, start : start + HEAD] = got.astype(BF16)
-    total = jnp.zeros((ROWS, WIDTH), F32)
+    attended = att_ref[...]
     for p in range(parts):
         copies[p].wait()
-        total = total + dot(
-            att_ref[:, p * depth : (p + 1) * depth], w_ref[p * depth : (p + 1) * depth, :]
-        )
-    mixed = total.astype(BF16)
-    mixed_ref[...] = mixed
-    wide = mixed.astype(F32)
+        mixed_ref[:, p * span : (p + 1) * span] = dot(attended, w_ref[p]).astype(BF16)
+    wide = mixed_ref[...].astype(F32)
     mean_square = jnp.mean(wide * wide, axis=1, keepdims=True)
     normed = wide * lax.rsqrt(mean_square + 1e-06) * gain_ref[...].astype(F32)
     for j in range(CHUNKS):
-        tall_ref[pl.ds(j, ROWS, stride=CHUNKS), :] = normed[:, j * 128 : (j + 1) * 128]
-    tile_ref[...] = tall_ref[...].astype(BF16).reshape(ROWS, CHUNKS, 128)
+        tall_ref[pl.ds(j, ROWS, stride=PITCH), :] = normed[:, j * 128 : (j + 1) * 128]
+    for t in range(ROWS):
+        tile_ref[t] = tall_ref[t * PITCH : t * PITCH + CHUNKS, :].astype(BF16)
     sends = out_sems.shape[0]
     share = DEVICES // sends
     outs = []
@@ -271,9 +282,11 @@
 
 
 def expert_kernel(
-    place_ref, slots_ref, x_ref, gate_hbm, up_hbm, down_hbm, router_ref, out_ref,
-    gate_ref, up_ref, down_ref, tall_ref, rows_ref, hidden_ref, back_ref, sems,
+    place_ref, slots_ref, x_hbm, gate_hbm, up_hbm, down_hbm, router_ref, out_ref,
+    x_ref, gate_ref, up_ref, down_ref, tall_ref, rows_ref, hidden_ref, sems,
 ):
+    arrival = pltpu.make_async_copy(x_hbm, x_ref, sems.at[3])
+    arrival.start()
     copies = [
         pltpu.make_async_copy(source.at[0], target, sems.at[n])
         for n, (source, target) in enumerate(
@@ -282,68 +295,41 @@
     ]
     for copy in copies:
         copy.start()
-    parts, half = rows_ref.shape[:2]
+    out_ref[...] = jnp.zeros(out_ref.shape, BF16)
+    arrival.wait()
     me = place_ref[0]
-
-    def take(part, begin, end):
-        for i in range(begin, end):
-            tall_ref[part, i * CHUNKS : (i + 1) * CHUNKS, :] = x_ref[
-                slots_ref[0, part * half + i]
-            ].astype(F32)
-
-    def flatten(part, begin, end):
-        for j in range(begin, end):
-            rows_ref[part, :, j * 128 : (j + 1) * 128] = tall_ref[
-                part, pl.ds(j, half, stride=CHUNKS), :
-            ].astype(BF16)
-
-    def put(part, begin, end):
-        for i in range(begin, end):
-            out_ref[slots_ref[0, part * half + i]] = back_ref[
-                part, i * CHUNKS : (i + 1) * CHUNKS, :
-            ].astype(BF16)
-
-    take(0, 0, half)
-    flatten(0, 0, CHUNKS)
+    for i in range(CHOSEN):
+        tall_ref[i * PITCH : i * PITCH + CHUNKS, :] = x_ref[slots_ref[0, i]].astype(F32)
+    for j in range(CHUNKS):
+        rows_ref[:, j * 128 : (j + 1) * 128] = tall_ref[pl.ds(j, CHOSEN, stride=PITCH), :].astype(BF16)
+    rows = rows_ref[...]
     wide = HIDDEN // 3
-    for part in range(parts):
-        for n in range(3):
-            columns = slice(n * wide, (n + 1) * wide)
-            if part == 0 and n == 0:
-                copies[0].wait()
-            gate = dot(rows_ref[part], gate_ref[:, columns])
-            if part == 0 and n == 0:
-                copies[1].wait()
-            up = dot(rows_ref[part], up_ref[:, columns])
-            if part == 0:
-                if n < 2:
-                    out_ref[n * SENT // 2 : (n + 1) * SENT // 2] = jnp.zeros(
-                        (SENT // 2, CHUNKS, 128), BF16
-                    )
-                    take(1, n * half // 2, (n + 1) * half // 2)
-                else:
-                    flatten(1, 0, CHUNKS)
-            else:
-                put(0, n * half // 3, (n + 1) * half // 3)
-            hidden_ref[part, :, columns] = (jax.nn.silu(gate) * up).astype(BF16)
-        logits = dot(rows_ref[part], router_ref[...])
-        mine = jnp.where(iota((half, 128), 1) == me, logits, 0.0)
-        weight = jax.nn.sigmoid(jnp.sum(mine, axis=1, keepdims=True))
-        if part == 0:
-            copies[2].wait()
-        for n in range(4):
-            result = dot(hidden_ref[part], down_ref[:, n * 512 : (n + 1) * 512]) * weight
-            for j in range(4):
-                back_ref[part, pl.ds(4 * n + j, half, stride=CHUNKS), :] = result[
-                    :, j * 128 : (j + 1) * 128
-                ]
-    put(1, 0, half)
+    for n in range(3):
+        columns = slice(n * wide, (n + 1) * wide)
+        if n == 0:
+            copies[0].wait()
+        gate = dot(rows, gate_ref[:, columns])
+        if n == 0:
+            copies[1].wait()
+        up = dot(rows, up_ref[:, columns])
+        hidden_ref[:, columns] = (jax.nn.silu(gate) * up).astype(BF16)
+    logits = dot(rows, router_ref[...])
+    mine = jnp.where(iota((CHOSEN, 128), 1) == me, logits, 0.0)
+    weight = jax.nn.sigmoid(jnp.sum(mine, axis=1, keepdims=True))
+    copies[2].wait()
+    hidden = hidden_ref[...]
+    for n in range(8):
+        result = dot(hidden, down_ref[:, n * 256 : (n + 1) * 256]) * weight
+        for j in range(2):
+            tall_ref[pl.ds(2 * n + j, CHOSEN, stride=PITCH), :] = result[:, j * 128 : (j + 1) * 128]
+    for i in range(CHOSEN):
+        out_ref[slots_ref[0, i]] = tall_ref[i * PITCH : i * PITCH + CHUNKS, :].astype(BF16)
 
 
 def combine_kernel(marks_ref, mixed_ref, x_ref, out_ref, tall_ref):
     for e in range(DEVICES):
         for k in range(ESLOTS):
-            start = (k * DEVICES + e) * CHUNKS
+            start = (k * DEVICES + e) * PITCH
             tall_ref[start : start + CHUNKS, :] = x_ref[e * ESLOTS + k].astype(F32)
     token = iota((ROWS, DEVICES), 0) + 1
     match = jnp.concatenate(
@@ -352,7 +338,7 @@
     for n in range(CHUNKS // 2):
         flat = jnp.concatenate(
             [
-                tall_ref[pl.ds(2 * n + j, SENT, stride=CHUNKS), :].astype(BF16)
+                tall_ref[pl.ds(2 * n + j, SENT, stride=PITCH), :].astype(BF16)
                 for j in range(2)
             ],
             axis=1,
@@ -392,7 +378,7 @@
 
     request = call(request_kernel, shape((DEVICES, 128), F32), [whole()])(cluster_lists)
     asked = exchange(request.reshape(DEVICES, 1, 128)).reshape(DEVICES, 128)
-    empty = call(empty_kernel, shape((2, PLACES, 128)), [whole()])(cluster_lists)
+    empty = call(empty_kernel, shape((2, 8, PLACES), F32), [whole()])(cluster_lists)
     marks, rows, slots = call(
         expert_index_kernel,
         (shape((8, DEVICES), I32), shape((8, DEVICES), I32), shape((1, CHOSEN), I32)),
@@ -403,14 +389,18 @@
         select_kernel,
         (shape((3, SEQ, 128), F32), shape((DEVICES, 9, 8, HEAD))),
         [whole(), whole()],
-    )(asked, near(qkv.transpose(1, 0, 2)))
+    )(asked, qkv.transpose(1, 0, 2))
     arrived = exchange(picked)
 
     outputs = call(
         attend_kernel,
         shape((DEVICES, 3, 8, HEAD)),
         [whole(), whole()],
-        [pltpu.VMEM((2, 3, PLACES, HEAD), BF16), pltpu.VMEM((GROWS, GROWS), F32)],
+        [
+            pltpu.VMEM((2, 3, PLACES, HEAD), BF16),
+            pltpu.VMEM((GROWS, GROWS), F32),
+            pltpu.VMEM((GROWS, HEAD), BF16),
+        ],
     )(empty, near(arrived))
     came_back = exchange(outputs)
 
@@ -419,9 +409,9 @@
         (shape((ROWS, WIDTH)), shape((SENT, CHUNKS, 128))),
         [smem, whole(), whole(), hbm, whole()],
         [
-            pltpu.VMEM((WIDTH, WIDTH), BF16),
+            pltpu.VMEM((4, WIDTH, WIDTH // 4), BF16),
             pltpu.VMEM((ROWS, WIDTH), BF16),
-            pltpu.VMEM((ROWS * CHUNKS, 128), F32),
+            pltpu.VMEM((ROWS * PITCH, 128), F32),
             pltpu.VMEM((ROWS, CHUNKS, 128), BF16),
             pltpu.VMEM((SENT, CHUNKS, 128), BF16),
             pltpu.SemaphoreType.DMA((4,)),
@@ -431,20 +421,19 @@
     )(rows, wanted, near(came_back), w_out, norm_gain.reshape(1, WIDTH))
     incoming = exchange(outgoing)
 
-    half = CHOSEN // 2
     produced = call(
         expert_kernel,
         shape((SENT, CHUNKS, 128)),
-        [smem, smem, whole(), hbm, hbm, hbm, whole()],
+        [smem, smem, hbm, hbm, hbm, hbm, whole()],
         [
+            pltpu.VMEM((SENT, CHUNKS, 128), BF16),
             pltpu.VMEM((WIDTH, HIDDEN), BF16),
             pltpu.VMEM((WIDTH, HIDDEN), BF16),
             pltpu.VMEM((HIDDEN, WIDTH), BF16),
-            pltpu.VMEM((2, half * CHUNKS, 128), F32),
-            pltpu.VMEM((2, half, WIDTH), BF16),
-            pltpu.VMEM((2, half, HIDDEN), BF16),
-            pltpu.VMEM((2, half * CHUNKS, 128), F32),
-            pltpu.SemaphoreType.DMA((3,)),
+            pltpu.VMEM((CHOSEN * PITCH, 128), F32),
+            pltpu.VMEM((CHOSEN, WIDTH), BF16),
+            pltpu.VMEM((CHOSEN, HIDDEN), BF16),
+            pltpu.SemaphoreType.DMA((4,)),
         ],
     )(place, slots, incoming, w_gate, w_up, w_down, router)
     results = exchange(produced)
@@ -453,7 +442,7 @@
         combine_kernel,
         shape((ROWS, WIDTH)),
         [whole(), whole(), whole()],
-        [pltpu.VMEM((SENT * CHUNKS, 128), F32)],
+        [pltpu.VMEM((SENT * PITCH, 128), F32)],
     )(marks, mixed, results)
 
 

time: 217 us -> 211 us (0.972)
  Pallas kernels: 47.5 us -> 42.5 us
    pallas_call x2, Pallas kernels: 17.4 us -> 15 us  [the longest x1 12.8 us: shards(): call(expert_kernel, shape((SENT, CHUNKS, 128)), [smem, smem, hbm, hbm, hb...]
where the time goes in v2:
time: 211 us
  blocking collectives  115 us (55%)
  waiting for transfers between devices  44.1 us (21%)
  Pallas kernels  42.5 us (20%)
  starting transfers between devices  9 us (4%)
    all_to_all x3, blocking collectives, exchange(): return lax.all_to_all(array, ALL, split_axis=0, concat_axis=0, tiled=True)  115 us
    all_to_all x2, waiting for transfers between devices, exchange(): return lax.all_to_all(array, ALL, split_axis=0, concat_axis=0, tiled=True)  44.1 us
    pallas_call x1, Pallas kernels, shards(): call(expert_kernel, shape((SENT, CHUNKS, 128)), [smem, smem, hbm, hbm, hb...  12.8 us
    all_to_all x2, starting transfers between devices, exchange(): return lax.all_to_all(array, ALL, split_axis=0, concat_axis=0, tiled=True)  9 us
    pallas_call x1, Pallas kernels, shards(): call(mix_kernel, (shape((ROWS, WIDTH)), shape((SENT, CHUNKS, 128))), [sme...  7.87 us
    pallas_call x1, Pallas kernels, shards(): call(attend_kernel, shape((DEVICES, 3, 8, HEAD)), [whole(), whole()], [pl...  7.65 us
  transfers between devices with their start and end apart: 2, of which 2 were waited for; matrix products, arithmetic and copies ran while one was open for 0% of the time, Pallas kernels for 2%

profile of v2, /device:TPU:1, one launch (start us, length us, event | category | flops | bytes accessed | tf_op | source)
XLA Modules:
  0.0 210.7 jit_solution(17504727387479131150)
XLA Ops:
  0.0 1.9 shard_map.92
  1.9 21.5 %all_to_all.25 = f32[128,1,128]{2,1,0:T(1,128)} all-to-all(f32[128,1,128]{2,1,0:T(1,128)} %bitcast.8), channel_id=1, replica_groups=mesh['seq'=8,'grp'=16] {'seq','grp'}, dimensions={0} | all-to-all | bytes 131072 | tf_op jit(solution)/shard_map/all_to_all | solution.py:366
  23.3 4.2 %shard_map.93 = (f32[3,8,128]{2,1,0:T(8,128)}, bf16[128,9,8,128]{3,2,1,0:T(8,128)(2,1)}) custom-call(f32[128,128]{1,0:T(8,128)} %bitcast.7, bf16[3,128,2048]{2,1,0:T(8,128)(2,1)} %bitcast.6), custom_call_target="tpu_custom_call" | custom-call | tf_op jit(solution)/shard_map/pallas_call | solution.py:388
  27.5 4.5 %all-to-all-start.1 = ((bf16[128,9,8,128]{3,2,1,0:T(8,128)(2,1)}), bf16[128,9,8,128]{3,2,1,0:T(8,128)(2,1)S(1)}, u32[]{:S(2)}, u32[]{:S(2)}) async-start(bf16[128,9,8,128]{3,2,1,0:T(8,128)(2,1)} %get-tuple-element.15), calls=%async_computation.1 | async-start | bytes 4718592 | tf_op jit(solution)/shard_map/all_to_all | solution.py:366
  32.0 0.0 copy-start
  32.0 2.1 %shard_map.94.empty_ref = f32[2,8,1536]{2,1,0:T(8,128)} custom-call(s32[2,1,1024]{2,1,0:T(1,128)} %lists_ref.5), custom_call_target="tpu_custom_call" | custom-call | tf_op jit(solution)/shard_map/pallas_call | solution.py:381
  34.2 30.5 %all-to-all-done.1.x_ref = bf16[128,9,8,128]{3,2,1,0:T(8,128)(2,1)S(1)} async-done(((bf16[128,9,8,128]{3,2,1,0:T(8,128)(2,1)}), bf16[128,9,8,128]{3,2,1,0:T(8,128)(2,1)S(1)}, u32[]{:S(2)}, u32[]{:S(2)}) %all-to-all-start.1) | async-done | bytes 2359328 | tf_op jit(solution)/shard_map/all_to_all | solution.py:366
  64.7 7.6 %shard_map.95 = bf16[128,3,8,128]{3,2,1,0:T(8,128)(2,1)} custom-call(f32[2,8,1536]{2,1,0:T(8,128)} %shard_map.94.empty_ref, bf16[128,9,8,128]{3,2,1,0:T(8,128)(2,1)S(1)} %all-to-all-done.1.x_ref), custom_call_target="tpu_custom_call" | custom-call | tf_op jit(solution)/shard_map/pallas_call | solution.py:395
  72.3 4.5 %all-to-all-start.2 = ((bf16[128,3,8,128]{3,2,1,0:T(8,128)(2,1)}), bf16[128,3,8,128]{3,2,1,0:T(8,128)(2,1)S(1)}, u32[]{:S(2)}, u32[]{:S(2)}) async-start(bf16[128,3,8,128]{3,2,1,0:T(8,128)(2,1)} %shard_map.95), calls=%async_computation.2 | async-start | bytes 1572864 | tf_op jit(solution)/shard_map/all_to_all | solution.py:366
  76.8 0.0 copy-done
  76.9 0.6 reshape.15.gain_ref
  77.5 1.9 shard_map.91
  79.4 13.5 %all-to-all-done.2.came_ref = bf16[128,3,8,128]{3,2,1,0:T(8,128)(2,1)S(1)} async-done(((bf16[128,3,8,128]{3,2,1,0:T(8,128)(2,1)}), bf16[128,3,8,128]{3,2,1,0:T(8,128)(2,1)S(1)}, u32[]{:S(2)}, u32[]{:S(2)}) %all-to-all-start.2) | async-done | bytes 786464 | tf_op jit(solution)/shard_map/all_to_all | solution.py:366
  92.9 7.9 %shard_map.96 = (bf16[128,2048]{1,0:T(8,128)(2,1)}, bf16[768,16,128]{2,1,0:T(8,128)(2,1)}) custom-call(s32[8,128]{1,0:T(8,128)} %get-tuple-element.13.rows_ref, f32[3,8,128]{2,1,0:T(8,128)} %get-tuple-element.14.wanted_ref, bf16[128,3,8,128]{3,2,1,0:T(8,128)(2,1)S(1)} %all-to-all-done.2.came_ref, bf16[2048,2048]{1,0:T(8,128)(2,1)} %w_out_ref.1, ...), custom_call_target="tpu_custom_call" | custom-call | tf_op jit(solution)/shard_map/pallas_call | solution.py:407
  100.8 46.9 %all_to_all.26.x_hbm = bf16[768,16,128]{2,1,0:T(8,128)(2,1)} all-to-all(bf16[768,16,128]{2,1,0:T(8,128)(2,1)} %get-tuple-element.18), channel_id=1, replica_groups=mesh['seq'=8,'grp'=16] {'seq','grp'}, dimensions={0} | all-to-all | bytes 6291456 | tf_op jit(solution)/shard_map/all_to_all | solution.py:366
  147.7 12.8 %shard_map.97 = bf16[768,16,128]{2,1,0:T(8,128)(2,1)} custom-call(s32[1]{0:T(128)} %bitcast.place_ref, s32[1,512]{1,0:T(1,128)} %get-tuple-element.17.slots_ref, bf16[768,16,128]{2,1,0:T(8,128)(2,1)} %all_to_all.26.x_hbm, bf16[1,2048,768]{2,1,0:T(8,128)(2,1)} %gate_hbm.1, bf16[1,2048,768]{2,1,0:T(8,128)(2,1)} %up_hbm.1, bf16[1,768,2048]{2,1,0:T(8,128)(2,1)} %down_hbm.1, ...), custom_call_target="tpu_custom_call" | custom-call | tf_op jit(solution)/shard_map/pallas_call | solution.py:424
  160.5 46.2 %all_to_all.27.x_ref = bf16[768,16,128]{2,1,0:T(8,128)(2,1)} all-to-all(bf16[768,16,128]{2,1,0:T(8,128)(2,1)} %shard_map.97), channel_id=1, replica_groups=mesh['seq'=8,'grp'=16] {'seq','grp'}, dimensions={0} | all-to-all | bytes 6291456 | tf_op jit(solution)/shard_map/all_to_all | solution.py:366
  206.7 4.0 %shard_map.98 = bf16[128,2048]{1,0:T(8,128)(2,1)} custom-call(s32[8,128]{1,0:T(8,128)} %get-tuple-element.12.marks_ref, bf16[128,2048]{1,0:T(8,128)(2,1)} %get-tuple-element.16.mixed_ref, bf16[768,16,128]{2,1,0:T(8,128)(2,1)} %all_to_all.27.x_ref), custom_call_target="tpu_custom_call" | custom-call | tf_op jit(solution)/shard_map/pallas_call | solution.py:441
Async XLA Ops:
  27.5 37.2 %all-to-all-start.1 = ((bf16[128,9,8,128]{3,2,1,0:T(8,128)(2,1)}), bf16[128,9,8,128]{3,2,1,0:T(8,128)(2,1)S(1)}, u32[]{:S(2)}, u32[]{:S(2)}) async-start(bf16[128,9,8,128]{3,2,1,0:T(8,128)(2,1)} %get-tuple-element.15), calls=%async_computation.1 | async-start | bytes 4718592 | tf_op jit(solution)/shard_map/all_to_all | solution.py:366
  32.0 44.8 %copy-start = (bf16[2048]{0:T(1024)(128)(2,1)S(1)}, bf16[2048]{0:T(1024)(128)(2,1)}, u32[]{:S(2)}) copy-start(bf16[2048]{0:T(1024)(128)(2,1)} %param.12) | copy-start | bytes 12292
  72.3 20.6 %all-to-all-start.2 = ((bf16[128,3,8,128]{3,2,1,0:T(8,128)(2,1)}), bf16[128,3,8,128]{3,2,1,0:T(8,128)(2,1)S(1)}, u32[]{:S(2)}, u32[]{:S(2)}) async-start(bf16[128,3,8,128]{3,2,1,0:T(8,128)(2,1)} %shard_map.95), calls=%async_computation.2 | async-start | bytes 1572864 | tf_op jit(solution)/shard_map/all_to_all | solution.py:366

commit v3 on v2

--- a/solution.py
+++ b/solution.py
@@ -129,7 +129,19 @@
     return wanted
 
 
-def select_kernel(asked_ref, qkv_ref, wanted_ref, out_ref):
+def select_kernel(asked_ref, qkv_hbm, wanted_ref, out_hbm, qkv_ref, out_ref, in_sems, out_sems):
+    parts = in_sems.shape[0]
+    share = SEQ // parts
+    width = WIDTH // parts
+    copies = [
+        pltpu.make_async_copy(
+            qkv_hbm.at[:, :, pl.ds(p * width, width)], qkv_ref.at[p], in_sems.at[p]
+        )
+        for p in range(parts)
+    ]
+    for copy in copies:
+        copy.start()
+    sends = []
     wanted = wanted_rows(asked_ref[...])
     for kind in range(3):
         wanted_ref[kind] = wanted[kind]
@@ -139,10 +151,12 @@
         peers = slice(s * GRP, (s + 1) * GRP)
         high_match = wanted[2][s : s + 1, :] == token
         high = jnp.zeros((128, 3 * HEAD), F32)
+        if s % share == 0:
+            copies[s // share].wait()
         for h in range(2):
-            start = (2 * s + h) * HEAD
+            start = (2 * (s % share) + h) * HEAD
             packed = jnp.concatenate(
-                [qkv_ref[c, :, start : start + HEAD] for c in range(3)], axis=1
+                [qkv_ref[s // share, c, :, start : start + HEAD] for c in range(3)], axis=1
             )
             low_match = jnp.where(wanted[h][s : s + 1, :] == token, 1.0, 0.0).astype(BF16)
             low = dot(low_match, packed, TN).astype(BF16)
@@ -153,6 +167,14 @@
         high = high.astype(BF16)
         for c in range(3):
             out_ref[peers, 6 + c] = high[:, c * HEAD : (c + 1) * HEAD].reshape(GRP, 8, HEAD)
+        if s % 2 == 1:
+            span = pl.ds((s - 1) * GRP, 2 * GRP)
+            sends.append(
+                pltpu.make_async_copy(out_ref.at[span], out_hbm.at[span], out_sems.at[s // 2])
+            )
+            sends[-1].start()
+    for send in sends:
+        send.wait()
 
 
 def attend_kernel(empty_ref, x_ref, out_ref, packed_ref, causal_ref, result_ref):
@@ -282,11 +304,9 @@
 
 
 def expert_kernel(
-    place_ref, slots_ref, x_hbm, gate_hbm, up_hbm, down_hbm, router_ref, out_ref,
-    x_ref, gate_ref, up_ref, down_ref, tall_ref, rows_ref, hidden_ref, sems,
+    place_ref, slots_ref, x_ref, gate_hbm, up_hbm, down_hbm, router_ref, out_hbm,
+    out_ref, gate_ref, up_ref, down_ref, tall_ref, rows_ref, hidden_ref, sems, send_sems,
 ):
-    arrival = pltpu.make_async_copy(x_hbm, x_ref, sems.at[3])
-    arrival.start()
     copies = [
         pltpu.make_async_copy(source.at[0], target, sems.at[n])
         for n, (source, target) in enumerate(
@@ -295,13 +315,12 @@
     ]
     for copy in copies:
         copy.start()
-    out_ref[...] = jnp.zeros(out_ref.shape, BF16)
-    arrival.wait()
     me = place_ref[0]
     for i in range(CHOSEN):
         tall_ref[i * PITCH : i * PITCH + CHUNKS, :] = x_ref[slots_ref[0, i]].astype(F32)
     for j in range(CHUNKS):
         rows_ref[:, j * 128 : (j + 1) * 128] = tall_ref[pl.ds(j, CHOSEN, stride=PITCH), :].astype(BF16)
+    out_ref[...] = jnp.zeros(out_ref.shape, BF16)
     rows = rows_ref[...]
     wide = HIDDEN // 3
     for n in range(3):
@@ -322,8 +341,16 @@
         result = dot(hidden, down_ref[:, n * 256 : (n + 1) * 256]) * weight
         for j in range(2):
             tall_ref[pl.ds(2 * n + j, CHOSEN, stride=PITCH), :] = result[:, j * 128 : (j + 1) * 128]
-    for i in range(CHOSEN):
-        out_ref[slots_ref[0, i]] = tall_ref[i * PITCH : i * PITCH + CHUNKS, :].astype(BF16)
+    edges = (0, CHOSEN // 4, CHOSEN // 2, 3 * CHOSEN // 4, SENT)
+    sends = []
+    for p in range(4):
+        for i in range(p * CHOSEN // 4, (p + 1) * CHOSEN // 4):
+            out_ref[slots_ref[0, i]] = tall_ref[i * PITCH : i * PITCH + CHUNKS, :].astype(BF16)
+        span = pl.ds(edges[p], edges[p + 1] - edges[p])
+        sends.append(pltpu.make_async_copy(out_ref.at[span], out_hbm.at[span], send_sems.at[p]))
+        sends[-1].start()
+    for send in sends:
+        send.wait()
 
 
 def combine_kernel(marks_ref, mixed_ref, x_ref, out_ref, tall_ref):
@@ -388,7 +415,14 @@
     wanted, picked = call(
         select_kernel,
         (shape((3, SEQ, 128), F32), shape((DEVICES, 9, 8, HEAD))),
-        [whole(), whole()],
+        [whole(), hbm],
+        [
+            pltpu.VMEM((2, 3, ROWS, WIDTH // 2), BF16),
+            pltpu.VMEM((DEVICES, 9, 8, HEAD), BF16),
+            pltpu.SemaphoreType.DMA((2,)),
+            pltpu.SemaphoreType.DMA((4,)),
+        ],
+        out_specs=(whole(), hbm),
     )(asked, qkv.transpose(1, 0, 2))
     arrived = exchange(picked)
 
@@ -424,7 +458,7 @@
     produced = call(
         expert_kernel,
         shape((SENT, CHUNKS, 128)),
-        [smem, smem, hbm, hbm, hbm, hbm, whole()],
+        [smem, smem, whole(), hbm, hbm, hbm, whole()],
         [
             pltpu.VMEM((SENT, CHUNKS, 128), BF16),
             pltpu.VMEM((WIDTH, HIDDEN), BF16),
@@ -433,9 +467,11 @@
             pltpu.VMEM((CHOSEN * PITCH, 128), F32),
             pltpu.VMEM((CHOSEN, WIDTH), BF16),
             pltpu.VMEM((CHOSEN, HIDDEN), BF16),
+            pltpu.SemaphoreType.DMA((3,)),
             pltpu.SemaphoreType.DMA((4,)),
         ],
-    )(place, slots, incoming, w_gate, w_up, w_down, router)
+        out_specs=hbm,
+    )(place, slots, near(incoming), w_gate, w_up, w_down, router)
     results = exchange(produced)
 
     return call(
@@ -443,7 +479,7 @@
         shape((ROWS, WIDTH)),
         [whole(), whole(), whole()],
         [pltpu.VMEM((SENT * PITCH, 128), F32)],
-    )(marks, mixed, results)
+    )(marks, mixed, near(results))
 
 
 def solution(mesh):

time: 211 us -> 208 us (0.986)
  no operation moved by 1% of the time
where the time goes in v3:
time: 208 us; the launch traced here: 207 us
  blocking collectives  113 us (54%)
  waiting for transfers between devices  44.1 us (21%)
  Pallas kernels  40.5 us (19%)
  starting transfers between devices  9.02 us (4%)
    all_to_all x3, blocking collectives, exchange(): return lax.all_to_all(array, ALL, split_axis=0, concat_axis=0, tiled=True)  113 us
    all_to_all x2, waiting for transfers between devices, exchange(): return lax.all_to_all(array, ALL, split_axis=0, concat_axis=0, tiled=True)  44.1 us
    pallas_call x1, Pallas kernels, shards(): call(expert_kernel, shape((SENT, CHUNKS, 128)), [smem, smem, whole(), hbm...  11.4 us
    all_to_all x2, starting transfers between devices, exchange(): return lax.all_to_all(array, ALL, split_axis=0, concat_axis=0, tiled=True)  9.02 us
    pallas_call x1, Pallas kernels, shards(): call(mix_kernel, (shape((ROWS, WIDTH)), shape((SENT, CHUNKS, 128))), [sme...  7.84 us
    pallas_call x1, Pallas kernels, shards(): call(attend_kernel, shape((DEVICES, 3, 8, HEAD)), [whole(), whole()], [pl...  7.64 us
    pallas_call x1, Pallas kernels, shards(): call(select_kernel, (shape((3, SEQ, 128), F32), shape((DEVICES, 9, 8, HEA...  4.69 us
  transfers between devices with their start and end apart: 2, of which 2 were waited for; matrix products, arithmetic and copies ran while one was open for 0% of the time, Pallas kernels for 2%

profile of v3, /device:TPU:1, one launch (start us, length us, event | category | flops | bytes accessed | tf_op | source)
XLA Modules:
  0.0 207.4 jit_solution(4436619463562164684)
XLA Ops:
  0.0 1.9 shard_map.92
  1.9 21.5 %all_to_all.25 = f32[128,1,128]{2,1,0:T(1,128)} all-to-all(f32[128,1,128]{2,1,0:T(1,128)} %bitcast.8), channel_id=1, replica_groups=mesh['seq'=8,'grp'=16] {'seq','grp'}, dimensions={0} | all-to-all | bytes 131072 | tf_op jit(solution)/shard_map/all_to_all | solution.py:393
  23.3 4.7 %shard_map.93 = (f32[3,8,128]{2,1,0:T(8,128)}, bf16[128,9,8,128]{3,2,1,0:T(8,128)(2,1)}) custom-call(f32[128,128]{1,0:T(8,128)} %bitcast.7, bf16[3,128,2048]{2,1,0:T(8,128)(2,1)} %bitcast.6), custom_call_target="tpu_custom_call" | custom-call | tf_op jit(solution)/shard_map/pallas_call | solution.py:415
  28.0 4.5 %all-to-all-start.1 = ((bf16[128,9,8,128]{3,2,1,0:T(8,128)(2,1)}), bf16[128,9,8,128]{3,2,1,0:T(8,128)(2,1)S(1)}, u32[]{:S(2)}, u32[]{:S(2)}) async-start(bf16[128,9,8,128]{3,2,1,0:T(8,128)(2,1)} %get-tuple-element.15), calls=%async_computation.1 | async-start | bytes 4718592 | tf_op jit(solution)/shard_map/all_to_all | solution.py:393
  32.6 0.0 copy-start
  32.6 2.1 %shard_map.94.empty_ref = f32[2,8,1536]{2,1,0:T(8,128)} custom-call(s32[2,1,1024]{2,1,0:T(1,128)} %lists_ref.5), custom_call_target="tpu_custom_call" | custom-call | tf_op jit(solution)/shard_map/pallas_call | solution.py:408
  34.7 30.5 %all-to-all-done.1.x_ref = bf16[128,9,8,128]{3,2,1,0:T(8,128)(2,1)S(1)} async-done(((bf16[128,9,8,128]{3,2,1,0:T(8,128)(2,1)}), bf16[128,9,8,128]{3,2,1,0:T(8,128)(2,1)S(1)}, u32[]{:S(2)}, u32[]{:S(2)}) %all-to-all-start.1) | async-done | bytes 2359328 | tf_op jit(solution)/shard_map/all_to_all | solution.py:393
  65.3 7.6 %shard_map.95 = bf16[128,3,8,128]{3,2,1,0:T(8,128)(2,1)} custom-call(f32[2,8,1536]{2,1,0:T(8,128)} %shard_map.94.empty_ref, bf16[128,9,8,128]{3,2,1,0:T(8,128)(2,1)S(1)} %all-to-all-done.1.x_ref), custom_call_target="tpu_custom_call" | custom-call | tf_op jit(solution)/shard_map/pallas_call | solution.py:429
  72.9 4.5 %all-to-all-start.2 = ((bf16[128,3,8,128]{3,2,1,0:T(8,128)(2,1)}), bf16[128,3,8,128]{3,2,1,0:T(8,128)(2,1)S(1)}, u32[]{:S(2)}, u32[]{:S(2)}) async-start(bf16[128,3,8,128]{3,2,1,0:T(8,128)(2,1)} %shard_map.95), calls=%async_computation.2 | async-start | bytes 1572864 | tf_op jit(solution)/shard_map/all_to_all | solution.py:393
  77.4 0.0 copy-done
  77.4 0.6 reshape.15.gain_ref
  78.0 1.9 shard_map.91
  80.0 13.5 %all-to-all-done.2.came_ref = bf16[128,3,8,128]{3,2,1,0:T(8,128)(2,1)S(1)} async-done(((bf16[128,3,8,128]{3,2,1,0:T(8,128)(2,1)}), bf16[128,3,8,128]{3,2,1,0:T(8,128)(2,1)S(1)}, u32[]{:S(2)}, u32[]{:S(2)}) %all-to-all-start.2) | async-done | bytes 786464 | tf_op jit(solution)/shard_map/all_to_all | solution.py:393
  93.5 7.8 %shard_map.96 = (bf16[128,2048]{1,0:T(8,128)(2,1)}, bf16[768,16,128]{2,1,0:T(8,128)(2,1)}) custom-call(s32[8,128]{1,0:T(8,128)} %get-tuple-element.13.rows_ref, f32[3,8,128]{2,1,0:T(8,128)} %get-tuple-element.14.wanted_ref, bf16[128,3,8,128]{3,2,1,0:T(8,128)(2,1)S(1)} %all-to-all-done.2.came_ref, bf16[2048,2048]{1,0:T(8,128)(2,1)} %w_out_ref.1, ...), custom_call_target="tpu_custom_call" | custom-call | tf_op jit(solution)/shard_map/pallas_call | solution.py:441
  101.3 46.2 %all_to_all.26.x_ref = bf16[768,16,128]{2,1,0:T(8,128)(2,1)S(1)} all-to-all(bf16[768,16,128]{2,1,0:T(8,128)(2,1)} %get-tuple-element.18), channel_id=1, replica_groups=mesh['seq'=8,'grp'=16] {'seq','grp'}, dimensions={0} | all-to-all | bytes 6291456 | tf_op jit(solution)/shard_map/all_to_all | solution.py:393
  147.5 11.4 %shard_map.97 = bf16[768,16,128]{2,1,0:T(8,128)(2,1)} custom-call(s32[1]{0:T(128)} %bitcast.place_ref, s32[1,512]{1,0:T(1,128)} %get-tuple-element.17.slots_ref, bf16[768,16,128]{2,1,0:T(8,128)(2,1)S(1)} %all_to_all.26.x_ref, bf16[1,2048,768]{2,1,0:T(8,128)(2,1)} %gate_hbm.1, bf16[1,2048,768]{2,1,0:T(8,128)(2,1)} %up_hbm.1, bf16[1,768,2048]{2,1,0:T(8,128)(2,1)} %down_hbm.1, ...), custom_call_target="tpu_custom_call" | custom-call | tf_op jit(solution)/shard_map/pallas_call | solution.py:458
  158.9 45.5 %all_to_all.27.x_ref = bf16[768,16,128]{2,1,0:T(8,128)(2,1)S(1)} all-to-all(bf16[768,16,128]{2,1,0:T(8,128)(2,1)} %shard_map.97), channel_id=1, replica_groups=mesh['seq'=8,'grp'=16] {'seq','grp'}, dimensions={0} | all-to-all | bytes 6291456 | tf_op jit(solution)/shard_map/all_to_all | solution.py:393
  204.4 3.0 %shard_map.98 = bf16[128,2048]{1,0:T(8,128)(2,1)} custom-call(s32[8,128]{1,0:T(8,128)} %get-tuple-element.12.marks_ref, bf16[128,2048]{1,0:T(8,128)(2,1)} %get-tuple-element.16.mixed_ref, bf16[768,16,128]{2,1,0:T(8,128)(2,1)S(1)} %all_to_all.27.x_ref), custom_call_target="tpu_custom_call" | custom-call | tf_op jit(solution)/shard_map/pallas_call | solution.py:477
Async XLA Ops:
  28.0 37.2 %all-to-all-start.1 = ((bf16[128,9,8,128]{3,2,1,0:T(8,128)(2,1)}), bf16[128,9,8,128]{3,2,1,0:T(8,128)(2,1)S(1)}, u32[]{:S(2)}, u32[]{:S(2)}) async-start(bf16[128,9,8,128]{3,2,1,0:T(8,128)(2,1)} %get-tuple-element.15), calls=%async_computation.1 | async-start | bytes 4718592 | tf_op jit(solution)/shard_map/all_to_all | solution.py:393
  32.6 44.8 %copy-start = (bf16[2048]{0:T(1024)(128)(2,1)S(1)}, bf16[2048]{0:T(1024)(128)(2,1)}, u32[]{:S(2)}) copy-start(bf16[2048]{0:T(1024)(128)(2,1)} %param.12) | copy-start | bytes 12292
  72.9 20.6 %all-to-all-start.2 = ((bf16[128,3,8,128]{3,2,1,0:T(8,128)(2,1)}), bf16[128,3,8,128]{3,2,1,0:T(8,128)(2,1)S(1)}, u32[]{:S(2)}, u32[]{:S(2)}) async-start(bf16[128,3,8,128]{3,2,1,0:T(8,128)(2,1)} %shard_map.95), calls=%async_computation.2 | async-start | bytes 1572864 | tf_op jit(solution)/shard_map/all_to_all | solution.py:393

commit v4 on v2

--- a/solution.py
+++ b/solution.py
@@ -28,6 +28,7 @@
 GROUP = 32
 FAR = -1e30
 PIECES = 3
+EARLY = 512
 PITCH = CHUNKS + 1
 GROWS = GROUP * SLOTS
 PLACES = DEVICES * SLOTS
@@ -48,6 +49,13 @@
 
 def whole(space=pltpu.VMEM):
     return pl.BlockSpec(memory_space=space)
+
+
+def fetch(pairs, sems):
+    copies = [pltpu.make_async_copy(a, b, sems.at[n]) for n, (a, b) in enumerate(pairs)]
+    for copy in copies:
+        copy.start()
+    return copies
 
 
 def rank_in_block(block, most):
@@ -94,7 +102,11 @@
         out_ref[h] = jnp.where(slot.astype(F32) < held, 0.0, FAR)
 
 
-def expert_index_kernel(place_ref, lists_ref, marks_ref, rows_ref, slots_ref):
+def expert_index_kernel(
+    place_ref, lists_ref, w_out_hbm, marks_ref, rows_ref, slots_ref, early_ref, sem
+):
+    early = pltpu.make_async_copy(w_out_hbm.at[:, pl.ds(0, EARLY)], early_ref, sem)
+    early.start()
     me = place_ref[0]
     lists = lists_ref[...]
     inside = (lists >> 7) == me
@@ -113,6 +125,7 @@
     mine = lists_ref[pl.ds(me, 1), :]
     block = mine >> 7
     slots_ref[...] = block * ESLOTS + rank_in_block(block, ESLOTS)
+    early.wait()
 
 
 def wanted_rows(asked):
@@ -129,10 +142,12 @@
     return wanted
 
 
-def select_kernel(asked_ref, qkv_ref, wanted_ref, out_ref):
+def select_kernel(asked_ref, qkv_hbm, wanted_ref, out_ref, qkv_ref, sems):
+    arrival = fetch([(qkv_hbm, qkv_ref)], sems)
     wanted = wanted_rows(asked_ref[...])
     for kind in range(3):
         wanted_ref[kind] = wanted[kind]
+    arrival[0].wait()
     token = (iota((ROWS, 128), 0) + 1).astype(F32)
     lane_head = (iota((ROWS, 128), 1) >> 2) & 1
     for s in range(SEQ):
@@ -230,17 +245,21 @@
 
 
 def mix_kernel(
-    rows_ref, wanted_ref, came_ref, w_out_ref, gain_ref, mixed_ref, out_hbm,
-    w_ref, att_ref, tall_ref, tile_ref, out_ref, w_sems, out_sems,
+    rows_hbm, wanted_hbm, came_ref, early_ref, w_out_ref, gain_hbm, mixed_ref, out_hbm,
+    rows_ref, wanted_ref, gain_ref, w_ref, att_ref, tall_ref, tile_ref, out_ref, w_sems, out_sems, sems,
 ):
     parts = w_sems.shape[0]
-    span = WIDTH // parts
+    span = (WIDTH - EARLY) // parts
     copies = [
-        pltpu.make_async_copy(w_out_ref.at[:, pl.ds(p * span, span)], w_ref.at[p], w_sems.at[p])
+        pltpu.make_async_copy(
+            w_out_ref.at[:, pl.ds(EARLY + p * span, span)], w_ref.at[p], w_sems.at[p]
+        )
         for p in range(parts)
     ]
     for copy in copies:
         copy.start()
+    small = fetch([(wanted_hbm, wanted_ref), (gain_hbm, gain_ref), (rows_hbm, rows_ref)], sems)
+    small[0].wait()
     token = (iota((ROWS, 128), 0) + 1).astype(F32)
     lane_head = (iota((ROWS, 128), 1) >> 2) & 1
     for s in range(SEQ):
@@ -257,9 +276,12 @@
             start = (2 * s + h) * HEAD
             att_ref[:, start : start + HEAD] = got.astype(BF16)
     attended = att_ref[...]
+    mixed_ref[:, :EARLY] = dot(attended, early_ref[...]).astype(BF16)
     for p in range(parts):
         copies[p].wait()
-        mixed_ref[:, p * span : (p + 1) * span] = dot(attended, w_ref[p]).astype(BF16)
+        mixed_ref[:, EARLY + p * span : EARLY + (p + 1) * span] = dot(attended, w_ref[p]).astype(BF16)
+    small[1].wait()
+    small[2].wait()
     wide = mixed_ref[...].astype(F32)
     mean_square = jnp.mean(wide * wide, axis=1, keepdims=True)
     normed = wide * lax.rsqrt(mean_square + 1e-06) * gain_ref[...].astype(F32)
@@ -282,55 +304,77 @@
 
 
 def expert_kernel(
-    place_ref, slots_ref, x_hbm, gate_hbm, up_hbm, down_hbm, router_ref, out_ref,
-    x_ref, gate_ref, up_ref, down_ref, tall_ref, rows_ref, hidden_ref, sems,
+    place_hbm, slots_hbm, x_ref, gate_hbm, up_hbm, down_hbm, router_hbm, out_hbm,
+    place_ref, slots_ref, router_ref, out_ref, gate_ref, up_ref, down_ref, tall_ref, rows_ref, hidden_ref, sems, send_sems, small_sems,
 ):
-    arrival = pltpu.make_async_copy(x_hbm, x_ref, sems.at[3])
-    arrival.start()
-    copies = [
-        pltpu.make_async_copy(source.at[0], target, sems.at[n])
-        for n, (source, target) in enumerate(
-            [(gate_hbm, gate_ref), (up_hbm, up_ref), (down_hbm, down_ref)]
-        )
-    ]
-    for copy in copies:
-        copy.start()
-    out_ref[...] = jnp.zeros(out_ref.shape, BF16)
-    arrival.wait()
+    wide = HIDDEN // 3
+    gates, ups = (
+        [
+            pltpu.make_async_copy(
+                source.at[0, :, pl.ds(n * wide, wide)], target.at[n], sems.at[first + n]
+            )
+            for n in range(3)
+        ]
+        for source, target, first in ((gate_hbm, gate_ref, 0), (up_hbm, up_ref, 3))
+    )
+    downs = pltpu.make_async_copy(down_hbm.at[0], down_ref, sems.at[6])
+    gates[0].start()
+    ups[0].start()
+    small = fetch([(place_hbm, place_ref), (slots_hbm, slots_ref)], small_sems)
+    late = pltpu.make_async_copy(router_hbm, router_ref, small_sems.at[2])
+    for copy in small:
+        copy.wait()
     me = place_ref[0]
     for i in range(CHOSEN):
         tall_ref[i * PITCH : i * PITCH + CHUNKS, :] = x_ref[slots_ref[0, i]].astype(F32)
+    gates[1].start()
+    ups[1].start()
     for j in range(CHUNKS):
         rows_ref[:, j * 128 : (j + 1) * 128] = tall_ref[pl.ds(j, CHOSEN, stride=PITCH), :].astype(BF16)
+    gates[2].start()
+    ups[2].start()
+    out_ref[...] = jnp.zeros(out_ref.shape, BF16)
+    downs.start()
+    late.start()
     rows = rows_ref[...]
-    wide = HIDDEN // 3
     for n in range(3):
         columns = slice(n * wide, (n + 1) * wide)
-        if n == 0:
-            copies[0].wait()
-        gate = dot(rows, gate_ref[:, columns])
-        if n == 0:
-            copies[1].wait()
-        up = dot(rows, up_ref[:, columns])
+        for part in ((0,), (1, 2), ())[n]:
+            gates[part].wait()
+            ups[part].wait()
+        gate = dot(rows, gate_ref[n])
+        up = dot(rows, up_ref[n])
         hidden_ref[:, columns] = (jax.nn.silu(gate) * up).astype(BF16)
+    late.wait()
+    downs.wait()
     logits = dot(rows, router_ref[...])
     mine = jnp.where(iota((CHOSEN, 128), 1) == me, logits, 0.0)
     weight = jax.nn.sigmoid(jnp.sum(mine, axis=1, keepdims=True))
-    copies[2].wait()
     hidden = hidden_ref[...]
     for n in range(8):
         result = dot(hidden, down_ref[:, n * 256 : (n + 1) * 256]) * weight
         for j in range(2):
             tall_ref[pl.ds(2 * n + j, CHOSEN, stride=PITCH), :] = result[:, j * 128 : (j + 1) * 128]
-    for i in range(CHOSEN):
-        out_ref[slots_ref[0, i]] = tall_ref[i * PITCH : i * PITCH + CHUNKS, :].astype(BF16)
-
-
-def combine_kernel(marks_ref, mixed_ref, x_ref, out_ref, tall_ref):
+    edges = (0, CHOSEN // 4, CHOSEN // 2, 3 * CHOSEN // 4, SENT)
+    sends = []
+    for p in range(4):
+        for i in range(p * CHOSEN // 4, (p + 1) * CHOSEN // 4):
+            out_ref[slots_ref[0, i]] = tall_ref[i * PITCH : i * PITCH + CHUNKS, :].astype(BF16)
+        span = pl.ds(edges[p], edges[p + 1] - edges[p])
+        sends.append(pltpu.make_async_copy(out_ref.at[span], out_hbm.at[span], send_sems.at[p]))
+        sends[-1].start()
+    for send in sends:
+        send.wait()
+
+
+def combine_kernel(marks_hbm, mixed_hbm, x_ref, out_ref, tall_ref, marks_ref, mixed_ref, sems):
+    small = fetch([(marks_hbm, marks_ref), (mixed_hbm, mixed_ref)], sems)
     for e in range(DEVICES):
         for k in range(ESLOTS):
             start = (k * DEVICES + e) * PITCH
             tall_ref[start : start + CHUNKS, :] = x_ref[e * ESLOTS + k].astype(F32)
+    for copy in small:
+        copy.wait()
     token = iota((ROWS, DEVICES), 0) + 1
     match = jnp.concatenate(
         [jnp.where(marks_ref[k : k + 1, :] == token, 1.0, 0.0) for k in range(ESLOTS)], axis=1
@@ -347,12 +391,16 @@
         out_ref[:, columns] = (mixed_ref[:, columns].astype(F32) + dot(match, flat)).astype(BF16)
 
 
+def specs_of(out_shape):
+    return tuple(whole() for _ in out_shape) if isinstance(out_shape, tuple) else whole()
+
+
 def call(kernel, out_shape, in_specs, scratch=(), out_specs=None):
     return pl.pallas_call(
         kernel,
         out_shape=out_shape,
         in_specs=in_specs,
-        out_specs=jax.tree.map(lambda _: whole(), out_shape) if out_specs is None else out_specs,
+        out_specs=specs_of(out_shape) if out_specs is None else out_specs,
         scratch_shapes=list(scratch),
         compiler_params=pltpu.CompilerParams(vmem_limit_bytes=VMEM_LIMIT),
     )
@@ -360,6 +408,10 @@
 
 def shape(dims, dtype=BF16):
     return jax.ShapeDtypeStruct(dims, dtype)
+
+
+def held(dims, dtype=BF16):
+    return pltpu.VMEM(dims, dtype)
 
 
 def exchange(array):
@@ -376,20 +428,27 @@
     smem = whole(pltpu.SMEM)
     hbm = whole(pl.ANY)
 
-    request = call(request_kernel, shape((DEVICES, 128), F32), [whole()])(cluster_lists)
+    request = call(request_kernel, held((DEVICES, 128), F32), [whole()])(cluster_lists)
     asked = exchange(request.reshape(DEVICES, 1, 128)).reshape(DEVICES, 128)
     empty = call(empty_kernel, shape((2, 8, PLACES), F32), [whole()])(cluster_lists)
-    marks, rows, slots = call(
+    marks, rows, slots, early = call(
         expert_index_kernel,
-        (shape((8, DEVICES), I32), shape((8, DEVICES), I32), shape((1, CHOSEN), I32)),
-        [smem, whole()],
-    )(place, expert_lists)
+        (
+            shape((8, DEVICES), I32),
+            shape((8, DEVICES), I32),
+            shape((1, CHOSEN), I32),
+            held((WIDTH, EARLY)),
+        ),
+        [smem, whole(), hbm],
+        [pltpu.SemaphoreType.DMA(())],
+    )(place, expert_lists, w_out)
 
     wanted, picked = call(
         select_kernel,
         (shape((3, SEQ, 128), F32), shape((DEVICES, 9, 8, HEAD))),
-        [whole(), whole()],
-    )(asked, qkv.transpose(1, 0, 2))
+        [whole(), hbm],
+        [pltpu.VMEM((3, ROWS, WIDTH), BF16), pltpu.SemaphoreType.DMA((1,))],
+    )(near(asked), qkv.transpose(1, 0, 2))
     arrived = exchange(picked)
 
     outputs = call(
@@ -407,43 +466,58 @@
     mixed, outgoing = call(
         mix_kernel,
         (shape((ROWS, WIDTH)), shape((SENT, CHUNKS, 128))),
-        [smem, whole(), whole(), hbm, whole()],
+        [hbm, hbm, whole(), whole(), hbm, hbm],
         [
-            pltpu.VMEM((4, WIDTH, WIDTH // 4), BF16),
+            pltpu.SMEM((8, DEVICES), I32),
+            pltpu.VMEM((3, SEQ, 128), F32),
+            pltpu.VMEM((1, WIDTH), BF16),
+            pltpu.VMEM((3, WIDTH, (WIDTH - EARLY) // 3), BF16),
             pltpu.VMEM((ROWS, WIDTH), BF16),
             pltpu.VMEM((ROWS * PITCH, 128), F32),
             pltpu.VMEM((ROWS, CHUNKS, 128), BF16),
             pltpu.VMEM((SENT, CHUNKS, 128), BF16),
+            pltpu.SemaphoreType.DMA((3,)),
             pltpu.SemaphoreType.DMA((4,)),
-            pltpu.SemaphoreType.DMA((4,)),
+            pltpu.SemaphoreType.DMA((3,)),
         ],
         out_specs=(whole(), hbm),
-    )(rows, wanted, near(came_back), w_out, norm_gain.reshape(1, WIDTH))
+    )(rows, wanted, near(came_back), near(early), w_out, norm_gain.reshape(1, WIDTH))
     incoming = exchange(outgoing)
 
     produced = call(
         expert_kernel,
         shape((SENT, CHUNKS, 128)),
-        [smem, smem, hbm, hbm, hbm, hbm, whole()],
+        [hbm, hbm, whole(), hbm, hbm, hbm, hbm],
         [
+            pltpu.SMEM((1,), I32),
+            pltpu.SMEM((1, CHOSEN), I32),
+            pltpu.VMEM((WIDTH, 128), BF16),
             pltpu.VMEM((SENT, CHUNKS, 128), BF16),
-            pltpu.VMEM((WIDTH, HIDDEN), BF16),
-            pltpu.VMEM((WIDTH, HIDDEN), BF16),
+            pltpu.VMEM((3, WIDTH, HIDDEN // 3), BF16),
+            pltpu.VMEM((3, WIDTH, HIDDEN // 3), BF16),
             pltpu.VMEM((HIDDEN, WIDTH), BF16),
             pltpu.VMEM((CHOSEN * PITCH, 128), F32),
             pltpu.VMEM((CHOSEN, WIDTH), BF16),
             pltpu.VMEM((CHOSEN, HIDDEN), BF16),
+            pltpu.SemaphoreType.DMA((7,)),
             pltpu.SemaphoreType.DMA((4,)),
+            pltpu.SemaphoreType.DMA((3,)),
         ],
-    )(place, slots, incoming, w_gate, w_up, w_down, router)
+        out_specs=hbm,
+    )(place, slots, near(incoming), w_gate, w_up, w_down, router)
     results = exchange(produced)
 
     return call(
         combine_kernel,
         shape((ROWS, WIDTH)),
-        [whole(), whole(), whole()],
-        [pltpu.VMEM((SENT * PITCH, 128), F32)],
-    )(marks, mixed, results)
+        [hbm, hbm, whole()],
+        [
+            pltpu.VMEM((SENT * PITCH, 128), F32),
+            pltpu.VMEM((8, DEVICES), I32),
+            pltpu.VMEM((ROWS, WIDTH), BF16),
+            pltpu.SemaphoreType.DMA((2,)),
+        ],
+    )(marks, mixed, near(results))
 
 
 def solution(mesh):

time: 211 us -> 203 us (0.962)
  Pallas kernels: 42.5 us -> 37.2 us
    pallas_call x4, Pallas kernels: 26.6 us -> 20.4 us  [the longest x1 10.4 us: shards(): call(expert_kernel, shape((SENT, CHUNKS, 128)), [hbm, hbm, whole(), hbm,...]
  transfers between devices with their start and end apart: 2 -> 2, of which waited for: 2 -> 2; matrix products, arithmetic and copies ran while one was open for 0% -> 0% of each run, Pallas kernels for 2% -> 3%
where the time goes in v4:
time: 203 us; the launch traced here: 202 us
  blocking collectives  113 us (56%)
  waiting for transfers between devices  42.8 us (21%)
  Pallas kernels  37.2 us (18%)
  starting transfers between devices  8.99 us (4%)
    all_to_all x3, blocking collectives, exchange(): return lax.all_to_all(array, ALL, split_axis=0, concat_axis=0, tiled=True)  113 us
    all_to_all x2, waiting for transfers between devices, exchange(): return lax.all_to_all(array, ALL, split_axis=0, concat_axis=0, tiled=True)  42.8 us
    pallas_call x1, Pallas kernels, shards(): call(expert_kernel, shape((SENT, CHUNKS, 128)), [hbm, hbm, whole(), hbm,...  10.4 us
    all_to_all x2, starting transfers between devices, exchange(): return lax.all_to_all(array, ALL, split_axis=0, concat_axis=0, tiled=True)  8.99 us
    pallas_call x1, Pallas kernels, shards(): call(attend_kernel, shape((DEVICES, 3, 8, HEAD)), [whole(), whole()], [pl...  7.65 us
    pallas_call x1, Pallas kernels, shards(): call(mix_kernel, (shape((ROWS, WIDTH)), shape((SENT, CHUNKS, 128))), [hbm...  6.39 us
  transfers between devices with their start and end apart: 2, of which 2 were waited for; matrix products, arithmetic and copies ran while one was open for 0% of the time, Pallas kernels for 3%

profile of v4, /device:TPU:1, one launch (start us, length us, event | category | flops | bytes accessed | tf_op | source)
XLA Modules:
  0.0 202.4 jit_solution(4404065934671285126)
XLA Ops:
  0.0 1.2 shard_map.92
  1.2 20.9 %all_to_all.25 = f32[128,1,128]{2,1,0:T(1,128)S(1)} all-to-all(f32[128,1,128]{2,1,0:T(1,128)S(1)} %bitcast.7), channel_id=1, replica_groups=mesh['seq'=8,'grp'=16] {'seq','grp'}, dimensions={0} | all-to-all | bytes 131072 | tf_op jit(solution)/shard_map/all_to_all | solution.py:418
  22.1 3.9 %shard_map.93 = (f32[3,8,128]{2,1,0:T(8,128)}, bf16[128,9,8,128]{3,2,1,0:T(8,128)(2,1)}) custom-call(f32[128,128]{1,0:T(8,128)S(1)} %bitcast.6, bf16[3,128,2048]{2,1,0:T(8,128)(2,1)} %bitcast.8), custom_call_target="tpu_custom_call" | custom-call | tf_op jit(solution)/shard_map/pallas_call | solution.py:446
  26.0 4.5 %all-to-all-start.1 = ((bf16[128,9,8,128]{3,2,1,0:T(8,128)(2,1)}), bf16[128,9,8,128]{3,2,1,0:T(8,128)(2,1)S(1)}, u32[]{:S(2)}, u32[]{:S(2)}) async-start(bf16[128,9,8,128]{3,2,1,0:T(8,128)(2,1)} %get-tuple-element.16), calls=%async_computation.1 | async-start | bytes 4718592 | tf_op jit(solution)/shard_map/all_to_all | solution.py:418
  30.5 0.0 copy-start
  30.5 2.1 %shard_map.94.empty_ref = f32[2,8,1536]{2,1,0:T(8,128)} custom-call(s32[2,1,1024]{2,1,0:T(1,128)} %lists_ref.5), custom_call_target="tpu_custom_call" | custom-call | tf_op jit(solution)/shard_map/pallas_call | solution.py:433
  32.7 30.5 %all-to-all-done.1.x_ref = bf16[128,9,8,128]{3,2,1,0:T(8,128)(2,1)S(1)} async-done(((bf16[128,9,8,128]{3,2,1,0:T(8,128)(2,1)}), bf16[128,9,8,128]{3,2,1,0:T(8,128)(2,1)S(1)}, u32[]{:S(2)}, u32[]{:S(2)}) %all-to-all-start.1) | async-done | bytes 2359328 | tf_op jit(solution)/shard_map/all_to_all | solution.py:418
  63.1 7.6 %shard_map.95 = bf16[128,3,8,128]{3,2,1,0:T(8,128)(2,1)} custom-call(f32[2,8,1536]{2,1,0:T(8,128)} %shard_map.94.empty_ref, bf16[128,9,8,128]{3,2,1,0:T(8,128)(2,1)S(1)} %all-to-all-done.1.x_ref), custom_call_target="tpu_custom_call" | custom-call | tf_op jit(solution)/shard_map/pallas_call | solution.py:454
  70.8 4.5 %all-to-all-start.2 = ((bf16[128,3,8,128]{3,2,1,0:T(8,128)(2,1)}), bf16[128,3,8,128]{3,2,1,0:T(8,128)(2,1)S(1)}, u32[]{:S(2)}, u32[]{:S(2)}) async-start(bf16[128,3,8,128]{3,2,1,0:T(8,128)(2,1)} %shard_map.95), calls=%async_computation.2 | async-start | bytes 1572864 | tf_op jit(solution)/shard_map/all_to_all | solution.py:418
  75.3 0.0 copy-done
  75.3 0.6 reshape.15.gain_hbm
  75.9 3.2 %shard_map.91 = (s32[8,128]{1,0:T(8,128)}, s32[8,128]{1,0:T(8,128)}, s32[1,512]{1,0:T(1,128)}, bf16[2048,512]{1,0:T(8,128)(2,1)S(1)}) custom-call(s32[1]{0:T(128)} %bitcast.place_ref.place_hbm, s32[128,512]{1,0:T(8,128)} %lists_ref.3, bf16[2048,2048]{1,0:T(8,128)(2,1)} %w_out_ref.1), custom_call_target="tpu_custom_call" | custom-call | tf_op jit(solution)/shard_map/pallas_call | solution.py:434
  79.1 12.3 %all-to-all-done.2.came_ref = bf16[128,3,8,128]{3,2,1,0:T(8,128)(2,1)S(1)} async-done(((bf16[128,3,8,128]{3,2,1,0:T(8,128)(2,1)}), bf16[128,3,8,128]{3,2,1,0:T(8,128)(2,1)S(1)}, u32[]{:S(2)}, u32[]{:S(2)}) %all-to-all-start.2) | async-done | bytes 786464 | tf_op jit(solution)/shard_map/all_to_all | solution.py:418
  91.4 6.4 %shard_map.96 = (bf16[128,2048]{1,0:T(8,128)(2,1)}, bf16[768,16,128]{2,1,0:T(8,128)(2,1)}) custom-call(s32[8,128]{1,0:T(8,128)} %get-tuple-element.14.rows_hbm, f32[3,8,128]{2,1,0:T(8,128)} %get-tuple-element.15.wanted_hbm, bf16[128,3,8,128]{3,2,1,0:T(8,128)(2,1)S(1)} %all-to-all-done.2.came_ref, bf16[2048,512]{1,0:T(8,128)(2,1)S(1)} %get-tuple-element.17.early_ref, ...), custom_call_target="tpu_custom_call" | custom-call | tf_op jit(solution)/shard_map/pallas_call | solution.py:466
  97.8 46.2 %all_to_all.26.x_ref = bf16[768,16,128]{2,1,0:T(8,128)(2,1)S(1)} all-to-all(bf16[768,16,128]{2,1,0:T(8,128)(2,1)} %get-tuple-element.20), channel_id=1, replica_groups=mesh['seq'=8,'grp'=16] {'seq','grp'}, dimensions={0} | all-to-all | bytes 6291456 | tf_op jit(solution)/shard_map/all_to_all | solution.py:418
  143.9 10.4 %shard_map.97 = bf16[768,16,128]{2,1,0:T(8,128)(2,1)} custom-call(s32[1]{0:T(128)} %bitcast.place_ref.place_hbm, s32[1,512]{1,0:T(1,128)} %get-tuple-element.19.slots_hbm, bf16[768,16,128]{2,1,0:T(8,128)(2,1)S(1)} %all_to_all.26.x_ref, bf16[1,2048,768]{2,1,0:T(8,128)(2,1)} %gate_hbm.1, bf16[1,2048,768]{2,1,0:T(8,128)(2,1)} %up_hbm.1, ...), custom_call_target="tpu_custom_call" | custom-call | tf_op jit(solution)/shard_map/pallas_call | solution.py:487
  154.3 45.5 %all_to_all.27.x_ref = bf16[768,16,128]{2,1,0:T(8,128)(2,1)S(1)} all-to-all(bf16[768,16,128]{2,1,0:T(8,128)(2,1)} %shard_map.97), channel_id=1, replica_groups=mesh['seq'=8,'grp'=16] {'seq','grp'}, dimensions={0} | all-to-all | bytes 6291456 | tf_op jit(solution)/shard_map/all_to_all | solution.py:418
  199.8 2.4 %shard_map.98 = bf16[128,2048]{1,0:T(8,128)(2,1)} custom-call(s32[8,128]{1,0:T(8,128)} %get-tuple-element.13.marks_hbm, bf16[128,2048]{1,0:T(8,128)(2,1)} %get-tuple-element.18.mixed_hbm, bf16[768,16,128]{2,1,0:T(8,128)(2,1)S(1)} %all_to_all.27.x_ref), custom_call_target="tpu_custom_call" | custom-call | tf_op jit(solution)/shard_map/pallas_call | solution.py:510
Async XLA Ops:
  26.0 37.1 %all-to-all-start.1 = ((bf16[128,9,8,128]{3,2,1,0:T(8,128)(2,1)}), bf16[128,9,8,128]{3,2,1,0:T(8,128)(2,1)S(1)}, u32[]{:S(2)}, u32[]{:S(2)}) async-start(bf16[128,9,8,128]{3,2,1,0:T(8,128)(2,1)} %get-tuple-element.16), calls=%async_computation.1 | async-start | bytes 4718592 | tf_op jit(solution)/shard_map/all_to_all | solution.py:418
  30.5 44.8 %copy-start = (bf16[2048]{0:T(1024)(128)(2,1)S(1)}, bf16[2048]{0:T(1024)(128)(2,1)}, u32[]{:S(2)}) copy-start(bf16[2048]{0:T(1024)(128)(2,1)} %param.12) | copy-start | bytes 12292
  70.8 20.6 %all-to-all-start.2 = ((bf16[128,3,8,128]{3,2,1,0:T(8,128)(2,1)}), bf16[128,3,8,128]{3,2,1,0:T(8,128)(2,1)S(1)}, u32[]{:S(2)}, u32[]{:S(2)}) async-start(bf16[128,3,8,128]{3,2,1,0:T(8,128)(2,1)} %shard_map.95), calls=%async_computation.2 | async-start | bytes 1572864 | tf_op jit(solution)/shard_map/all_to_all | solution.py:418

commit v5 on v4

--- a/solution.py
+++ b/solution.py
@@ -245,8 +245,8 @@
 
 
 def mix_kernel(
-    rows_hbm, wanted_hbm, came_ref, early_ref, w_out_ref, gain_hbm, mixed_ref, out_hbm,
-    rows_ref, wanted_ref, gain_ref, w_ref, att_ref, tall_ref, tile_ref, out_ref, w_sems, out_sems, sems,
+    rows_hbm, wanted_hbm, came_ref, early_ref, w_out_ref, gain_hbm, mixed_ref, out_ref,
+    rows_ref, wanted_ref, gain_ref, w_ref, att_ref, tall_ref, tile_ref, w_sems, sems,
 ):
     parts = w_sems.shape[0]
     span = (WIDTH - EARLY) // parts
@@ -289,18 +289,9 @@
         tall_ref[pl.ds(j, ROWS, stride=PITCH), :] = normed[:, j * 128 : (j + 1) * 128]
     for t in range(ROWS):
         tile_ref[t] = tall_ref[t * PITCH : t * PITCH + CHUNKS, :].astype(BF16)
-    sends = out_sems.shape[0]
-    share = DEVICES // sends
-    outs = []
-    for p in range(sends):
-        for e in range(p * share, (p + 1) * share):
-            for k in range(ESLOTS):
-                out_ref[e * ESLOTS + k] = tile_ref[rows_ref[k, e]]
-        span = pl.ds(p * share * ESLOTS, share * ESLOTS)
-        outs.append(pltpu.make_async_copy(out_ref.at[span], out_hbm.at[span], out_sems.at[p]))
-        outs[-1].start()
-    for copy in outs:
-        copy.wait()
+    for e in range(DEVICES):
+        for k in range(ESLOTS):
+            out_ref[e * ESLOTS + k] = tile_ref[rows_ref[k, e]]
 
 
 def expert_kernel(
@@ -475,12 +466,9 @@
             pltpu.VMEM((ROWS, WIDTH), BF16),
             pltpu.VMEM((ROWS * PITCH, 128), F32),
             pltpu.VMEM((ROWS, CHUNKS, 128), BF16),
-            pltpu.VMEM((SENT, CHUNKS, 128), BF16),
             pltpu.SemaphoreType.DMA((3,)),
-            pltpu.SemaphoreType.DMA((4,)),
             pltpu.SemaphoreType.DMA((3,)),
         ],
-        out_specs=(whole(), hbm),
     )(rows, wanted, near(came_back), near(early), w_out, norm_gain.reshape(1, WIDTH))
     incoming = exchange(outgoing)
 

time: 203 us -> 203 us (level)
  no operation moved by 1% of the time
where the time goes in v5:
time: 203 us; the launch traced here: 202 us
  blocking collectives  113 us (56%)
  waiting for transfers between devices  42.8 us (21%)
  Pallas kernels  37 us (18%)
  starting transfers between devices  8.99 us (4%)
    all_to_all x3, blocking collectives, exchange(): return lax.all_to_all(array, ALL, split_axis=0, concat_axis=0, tiled=True)  113 us
    all_to_all x2, waiting for transfers between devices, exchange(): return lax.all_to_all(array, ALL, split_axis=0, concat_axis=0, tiled=True)  42.8 us
    pallas_call x1, Pallas kernels, shards(): call(expert_kernel, shape((SENT, CHUNKS, 128)), [hbm, hbm, whole(), hbm,...  10.4 us
    all_to_all x2, starting transfers between devices, exchange(): return lax.all_to_all(array, ALL, split_axis=0, concat_axis=0, tiled=True)  8.99 us
    pallas_call x1, Pallas kernels, shards(): call(attend_kernel, shape((DEVICES, 3, 8, HEAD)), [whole(), whole()], [pl...  7.65 us
    pallas_call x1, Pallas kernels, shards(): call(mix_kernel, (shape((ROWS, WIDTH)), shape((SENT, CHUNKS, 128))), [hbm...  6.18 us
  transfers between devices with their start and end apart: 2, of which 2 were waited for; matrix products, arithmetic and copies ran while one was open for 0% of the time, Pallas kernels for 3%

profile of v5, /device:TPU:1, one launch (start us, length us, event | category | flops | bytes accessed | tf_op | source)
XLA Modules:
  0.0 202.2 jit_solution(17368887901837348864)
XLA Ops:
  0.0 1.2 shard_map.92
  1.2 20.9 %all_to_all.25 = f32[128,1,128]{2,1,0:T(1,128)S(1)} all-to-all(f32[128,1,128]{2,1,0:T(1,128)S(1)} %bitcast.7), channel_id=1, replica_groups=mesh['seq'=8,'grp'=16] {'seq','grp'}, dimensions={0} | all-to-all | bytes 131072 | tf_op jit(solution)/shard_map/all_to_all | solution.py:409
  22.1 3.9 %shard_map.93 = (f32[3,8,128]{2,1,0:T(8,128)}, bf16[128,9,8,128]{3,2,1,0:T(8,128)(2,1)}) custom-call(f32[128,128]{1,0:T(8,128)S(1)} %bitcast.6, bf16[3,128,2048]{2,1,0:T(8,128)(2,1)} %bitcast.8), custom_call_target="tpu_custom_call" | custom-call | tf_op jit(solution)/shard_map/pallas_call | solution.py:437
  26.0 4.5 %all-to-all-start.1 = ((bf16[128,9,8,128]{3,2,1,0:T(8,128)(2,1)}), bf16[128,9,8,128]{3,2,1,0:T(8,128)(2,1)S(1)}, u32[]{:S(2)}, u32[]{:S(2)}) async-start(bf16[128,9,8,128]{3,2,1,0:T(8,128)(2,1)} %get-tuple-element.16), calls=%async_computation.1 | async-start | bytes 4718592 | tf_op jit(solution)/shard_map/all_to_all | solution.py:409
  30.5 0.0 copy-start
  30.5 2.1 %shard_map.94.empty_ref = f32[2,8,1536]{2,1,0:T(8,128)} custom-call(s32[2,1,1024]{2,1,0:T(1,128)} %lists_ref.5), custom_call_target="tpu_custom_call" | custom-call | tf_op jit(solution)/shard_map/pallas_call | solution.py:424
  32.7 30.5 %all-to-all-done.1.x_ref = bf16[128,9,8,128]{3,2,1,0:T(8,128)(2,1)S(1)} async-done(((bf16[128,9,8,128]{3,2,1,0:T(8,128)(2,1)}), bf16[128,9,8,128]{3,2,1,0:T(8,128)(2,1)S(1)}, u32[]{:S(2)}, u32[]{:S(2)}) %all-to-all-start.1) | async-done | bytes 2359328 | tf_op jit(solution)/shard_map/all_to_all | solution.py:409
  63.1 7.6 %shard_map.95 = bf16[128,3,8,128]{3,2,1,0:T(8,128)(2,1)} custom-call(f32[2,8,1536]{2,1,0:T(8,128)} %shard_map.94.empty_ref, bf16[128,9,8,128]{3,2,1,0:T(8,128)(2,1)S(1)} %all-to-all-done.1.x_ref), custom_call_target="tpu_custom_call" | custom-call | tf_op jit(solution)/shard_map/pallas_call | solution.py:445
  70.8 4.5 %all-to-all-start.2 = ((bf16[128,3,8,128]{3,2,1,0:T(8,128)(2,1)}), bf16[128,3,8,128]{3,2,1,0:T(8,128)(2,1)S(1)}, u32[]{:S(2)}, u32[]{:S(2)}) async-start(bf16[128,3,8,128]{3,2,1,0:T(8,128)(2,1)} %shard_map.95), calls=%async_computation.2 | async-start | bytes 1572864 | tf_op jit(solution)/shard_map/all_to_all | solution.py:409
  75.3 0.0 copy-done
  75.3 0.6 reshape.15.gain_hbm
  75.9 3.2 %shard_map.91 = (s32[8,128]{1,0:T(8,128)}, s32[8,128]{1,0:T(8,128)}, s32[1,512]{1,0:T(1,128)}, bf16[2048,512]{1,0:T(8,128)(2,1)S(1)}) custom-call(s32[1]{0:T(128)} %bitcast.place_ref.place_hbm, s32[128,512]{1,0:T(8,128)} %lists_ref.3, bf16[2048,2048]{1,0:T(8,128)(2,1)} %w_out_ref.1), custom_call_target="tpu_custom_call" | custom-call | tf_op jit(solution)/shard_map/pallas_call | solution.py:425
  79.1 12.3 %all-to-all-done.2.came_ref = bf16[128,3,8,128]{3,2,1,0:T(8,128)(2,1)S(1)} async-done(((bf16[128,3,8,128]{3,2,1,0:T(8,128)(2,1)}), bf16[128,3,8,128]{3,2,1,0:T(8,128)(2,1)S(1)}, u32[]{:S(2)}, u32[]{:S(2)}) %all-to-all-start.2) | async-done | bytes 786464 | tf_op jit(solution)/shard_map/all_to_all | solution.py:409
  91.4 6.2 %shard_map.96 = (bf16[128,2048]{1,0:T(8,128)(2,1)}, bf16[768,16,128]{2,1,0:T(8,128)(2,1)}) custom-call(s32[8,128]{1,0:T(8,128)} %get-tuple-element.14.rows_hbm, f32[3,8,128]{2,1,0:T(8,128)} %get-tuple-element.15.wanted_hbm, bf16[128,3,8,128]{3,2,1,0:T(8,128)(2,1)S(1)} %all-to-all-done.2.came_ref, bf16[2048,512]{1,0:T(8,128)(2,1)S(1)} %get-tuple-element.17.early_ref, ...), custom_call_target="tpu_custom_call" | custom-call | tf_op jit(solution)/shard_map/pallas_call | solution.py:457
  97.6 46.2 %all_to_all.26.x_ref = bf16[768,16,128]{2,1,0:T(8,128)(2,1)S(1)} all-to-all(bf16[768,16,128]{2,1,0:T(8,128)(2,1)} %get-tuple-element.20), channel_id=1, replica_groups=mesh['seq'=8,'grp'=16] {'seq','grp'}, dimensions={0} | all-to-all | bytes 6291456 | tf_op jit(solution)/shard_map/all_to_all | solution.py:409
  143.7 10.4 %shard_map.97 = bf16[768,16,128]{2,1,0:T(8,128)(2,1)} custom-call(s32[1]{0:T(128)} %bitcast.place_ref.place_hbm, s32[1,512]{1,0:T(1,128)} %get-tuple-element.19.slots_hbm, bf16[768,16,128]{2,1,0:T(8,128)(2,1)S(1)} %all_to_all.26.x_ref, bf16[1,2048,768]{2,1,0:T(8,128)(2,1)} %gate_hbm.1, bf16[1,2048,768]{2,1,0:T(8,128)(2,1)} %up_hbm.1, ...), custom_call_target="tpu_custom_call" | custom-call | tf_op jit(solution)/shard_map/pallas_call | solution.py:475
  154.1 45.5 %all_to_all.27.x_ref = bf16[768,16,128]{2,1,0:T(8,128)(2,1)S(1)} all-to-all(bf16[768,16,128]{2,1,0:T(8,128)(2,1)} %shard_map.97), channel_id=1, replica_groups=mesh['seq'=8,'grp'=16] {'seq','grp'}, dimensions={0} | all-to-all | bytes 6291456 | tf_op jit(solution)/shard_map/all_to_all | solution.py:409
  199.6 2.4 %shard_map.98 = bf16[128,2048]{1,0:T(8,128)(2,1)} custom-call(s32[8,128]{1,0:T(8,128)} %get-tuple-element.13.marks_hbm, bf16[128,2048]{1,0:T(8,128)(2,1)} %get-tuple-element.18.mixed_hbm, bf16[768,16,128]{2,1,0:T(8,128)(2,1)S(1)} %all_to_all.27.x_ref), custom_call_target="tpu_custom_call" | custom-call | tf_op jit(solution)/shard_map/pallas_call | solution.py:498
Async XLA Ops:
  26.0 37.1 %all-to-all-start.1 = ((bf16[128,9,8,128]{3,2,1,0:T(8,128)(2,1)}), bf16[128,9,8,128]{3,2,1,0:T(8,128)(2,1)S(1)}, u32[]{:S(2)}, u32[]{:S(2)}) async-start(bf16[128,9,8,128]{3,2,1,0:T(8,128)(2,1)} %get-tuple-element.16), calls=%async_computation.1 | async-start | bytes 4718592 | tf_op jit(solution)/shard_map/all_to_all | solution.py:409
  30.5 44.8 %copy-start = (bf16[2048]{0:T(1024)(128)(2,1)S(1)}, bf16[2048]{0:T(1024)(128)(2,1)}, u32[]{:S(2)}) copy-start(bf16[2048]{0:T(1024)(128)(2,1)} %param.12) | copy-start | bytes 12292
  70.8 20.6 %all-to-all-start.2 = ((bf16[128,3,8,128]{3,2,1,0:T(8,128)(2,1)}), bf16[128,3,8,128]{3,2,1,0:T(8,128)(2,1)S(1)}, u32[]{:S(2)}, u32[]{:S(2)}) async-start(bf16[128,3,8,128]{3,2,1,0:T(8,128)(2,1)} %shard_map.95), calls=%async_computation.2 | async-start | bytes 1572864 | tf_op jit(solution)/shard_map/all_to_all | solution.py:409
